TPU v7x, 32 devices: a whole 2x2x4 slice. The times are simulated.
32 devices in a mesh: img: 16 (over z, y, x), lat: 2 (over core).
Axes of the slice: x: 2, y: 2, z: 4, core: 2. Of those that a mesh axis runs over, the one named last changes fastest.
Arguments:
- media_tokens: bfloat16 [80, 256, 1024], P('img', 'lat'), may hold values from -6 to 6
- image_counts: int32 [16], P('img'), may hold values from 1 to 5
- latent_init: bfloat16 [64, 1024], P('lat'), may hold values from -6 to 6
- cotangent: bfloat16 [80, 64, 1024], P('img', 'lat'), may hold values from -6 to 6
- query_weight: bfloat16 [2, 1024, 512], P(None, ('img', 'lat')), may hold values from -0.1875 to 0.1875
- key_value_weight: bfloat16 [2, 1024, 1024], P(None, ('img', 'lat')), may hold values from -0.1875 to 0.1875
- output_weight: bfloat16 [2, 512, 1024], P(None, ('img', 'lat')), may hold values from -0.75 to 0.75
- up_weight: bfloat16 [2, 1024, 4096], P(None, ('img', 'lat')), may hold values from -0.1875 to 0.1875
- down_weight: bfloat16 [2, 4096, 1024], P(None, ('img', 'lat')), may hold values from -0.09375 to 0.09375
- norm_gain: bfloat16 [2, 3, 1024], P(None, None, ('img', 'lat')), may hold values from 0.5 to 1.5
- norm_shift: bfloat16 [2, 3, 1024], P(None, None, ('img', 'lat')), may hold values from -1.75 to 1.75
Outputs:
- resampled: float32 [80, 64, 1024], P('img', 'lat')
- media_grad: float32 [80, 256, 1024], P('img', 'lat')
- latent_grad: float32 [64, 1024], P('lat')
- query_grad: float32 [2, 1024, 512], P(None, ('img', 'lat'))
- key_value_grad: float32 [2, 1024, 1024], P(None, ('img', 'lat'))
- output_grad: float32 [2, 512, 1024], P(None, ('img', 'lat'))
- up_grad: float32 [2, 1024, 4096], P(None, ('img', 'lat'))
- down_grad: float32 [2, 4096, 1024], P(None, ('img', 'lat'))
- gain_grad: float32 [2, 3, 1024], P(None, None, ('img', 'lat'))
- shift_grad: float32 [2, 3, 1024], P(None, None, ('img', 'lat'))
Inputs may be any that keep to these rules, and one draw needn't show every extreme that they name: image_counts[b] is the number of sample b's 5 slots that hold an image: slot j of it is filled when j < image_counts[b], the rest are padding.
All inputs are finite; a program needn't handle non-finite values.
Results may differ from a plain program's by a relative error of at most 0.019.
Values may be sent and summed in bfloat16 or wider, within the bound.
No kernel may reach another device: no remote copies, remote signals or barrier semaphores. Data moves between devices by JAX's collectives and lax.ppermute only.
A program may use at most 320 MiB of HBM per device.

v0:
```python
import jax
import jax.numpy as jnp
from jax import lax
from jax.sharding import PartitionSpec as P

HEAD = 64
MEDIA = 5
LAYERS = 2


def norm_rows(inputs, scale_row, shift_row):
    average = jnp.mean(inputs, axis=-1, keepdims=True)
    centered = inputs - average
    variance = jnp.mean(centered * centered, axis=-1, keepdims=True)
    return centered * lax.rsqrt(variance + 1e-05) * scale_row + shift_row


def layer_forward(latent_rows, media_float, current):
    (
        query_projection_weight,
        key_value_w,
        output_projection_weight,
        up_projection_weight,
        down_projection_weight,
        gains,
        shifts,
    ) = current
    gain_rows = gains.astype(jnp.float32)
    shift_rows = shifts.astype(jnp.float32)
    inner_width = query_projection_weight.shape[1]
    head_count = inner_width // HEAD
    slot_count = latent_rows.shape[0]
    query_rows = latent_rows.shape[1]
    media_norm = norm_rows(media_float, gain_rows[0], shift_rows[0]).astype(jnp.bfloat16)
    normed_latent_rows = norm_rows(latent_rows, gain_rows[1], shift_rows[1]).astype(jnp.bfloat16)
    query = jnp.einsum(
        "pam,mn->pan",
        normed_latent_rows,
        query_projection_weight,
        preferred_element_type=jnp.float32,
    ).astype(jnp.bfloat16)
    joined = jnp.concatenate([media_norm, normed_latent_rows], axis=1)
    own_pairs = jnp.einsum(
        "skd,de->ske", joined, key_value_w, preferred_element_type=jnp.float32
    ).astype(jnp.bfloat16)
    key_value = lax.all_gather(own_pairs, "lat", axis=1, tiled=True)
    key_rows = key_value.shape[1]
    query_heads = query.reshape(slot_count, query_rows, head_count, HEAD)
    key_heads = key_value[..., :inner_width].reshape(slot_count, key_rows, head_count, HEAD)
    value_heads = key_value[..., inner_width:].reshape(slot_count, key_rows, head_count, HEAD)
    scores = (
        jnp.einsum("sqhe,skhe->shqk", query_heads, key_heads, preferred_element_type=jnp.float32)
        * 0.125
    )
    row_max = jnp.max(scores, axis=-1, keepdims=True)
    exponent = jnp.exp(scores - row_max)
    totals = jnp.sum(exponent, axis=-1, keepdims=True)
    probs = (exponent / totals).astype(jnp.bfloat16)
    log_total = row_max + jnp.log(totals)
    mixed_rows = jnp.einsum(
        "shqk,skhe->sqhe", probs, value_heads, preferred_element_type=jnp.float32
    )
    mixed_rows = mixed_rows.reshape(slot_count, query_rows, inner_width).astype(jnp.bfloat16)
    residual_after = latent_rows + jnp.einsum(
        "pam,mn->pan", mixed_rows, output_projection_weight, preferred_element_type=jnp.float32
    )
    normalized_rows = norm_rows(residual_after, gain_rows[2], shift_rows[2]).astype(jnp.bfloat16)
    hidden_rows = jnp.einsum(
        "cum,mz->cuz", normalized_rows, up_projection_weight, preferred_element_type=jnp.float32
    )
    activated_rows = jax.nn.gelu(hidden_rows, approximate=False).astype(jnp.bfloat16)
    layer_result = residual_after + jnp.einsum(
        "eqo,oz->eqz", activated_rows, down_projection_weight, preferred_element_type=jnp.float32
    )
    stored = (
        latent_rows,
        joined,
        query_heads,
        key_heads,
        value_heads,
        log_total,
        mixed_rows,
        residual_after,
        normalized_rows,
        hidden_rows,
        activated_rows,
    )
    return (layer_result, stored)


def layer_backward(upstream, media_float, current, stored):
    (
        query_projection_weight,
        key_value_w,
        output_projection_weight,
        up_projection_weight,
        down_projection_weight,
        gains,
        shifts,
    ) = current
    gain_rows = gains.astype(jnp.float32)
    shift_rows = shifts.astype(jnp.float32)
    (
        latent_rows,
        joined,
        query_heads,
        key_heads,
        value_heads,
        log_total,
        mixed_rows,
        residual_after,
        normalized_rows,
        hidden_rows,
        activated_rows,
    ) = stored
    inner_width = query_projection_weight.shape[1]
    slot_count = latent_rows.shape[0]
    query_rows = latent_rows.shape[1]
    patch_rows = media_float.shape[1]
    key_rows = key_heads.shape[1]
    head_count = inner_width // HEAD
    branch_gradient = upstream.astype(jnp.bfloat16)
    down_contribution = jnp.einsum(
        "wro,wrq->oq", activated_rows, branch_gradient, preferred_element_type=jnp.float32
    )
    down_summed = lax.psum_scatter(
        down_contribution, ("img", "lat"), scatter_dimension=0, tiled=True
    )
    activated_grad = jnp.einsum(
        "bzh,th->bzt", branch_gradient, down_projection_weight, preferred_element_type=jnp.float32
    )
    _, gelu_pull = jax.vjp(lambda inputs: jax.nn.gelu(inputs, approximate=False), hidden_rows)
    hidden_grad = gelu_pull(activated_grad)[0].astype(jnp.bfloat16)
    up_contribution = jnp.einsum(
        "aqj,aqm->jm", normalized_rows, hidden_grad, preferred_element_type=jnp.float32
    )
    up_summed = lax.psum_scatter(up_contribution, ("img", "lat"), scatter_dimension=0, tiled=True)
    normed_grad = jnp.einsum(
        "xrm,im->xri", hidden_grad, up_projection_weight, preferred_element_type=jnp.float32
    )
    _, feed_pull = jax.vjp(norm_rows, residual_after, gain_rows[2], shift_rows[2])
    d_after, gain_feed, shift_feed = feed_pull(normed_grad)
    d_after = d_after + upstream
    attention_branch_output = d_after.astype(jnp.bfloat16)
    output_term = jnp.einsum(
        "jmk,jmw->kw", mixed_rows, attention_branch_output, preferred_element_type=jnp.float32
    )
    mixed_grad = jnp.einsum(
        "nra,xa->nrx",
        attention_branch_output,
        output_projection_weight,
        preferred_element_type=jnp.float32,
    )
    mixed_grad = mixed_grad.astype(jnp.bfloat16).reshape(slot_count, query_rows, head_count, HEAD)
    scores = (
        jnp.einsum("sqhe,skhe->shqk", query_heads, key_heads, preferred_element_type=jnp.float32)
        * 0.125
    )
    soft = jnp.exp(scores - log_total)
    probs = soft.astype(jnp.bfloat16)
    d_probs = jnp.einsum(
        "sqhe,skhe->shqk", mixed_grad, value_heads, preferred_element_type=jnp.float32
    )
    d_values = jnp.einsum("shqk,sqhe->skhe", probs, mixed_grad, preferred_element_type=jnp.float32)
    d_scores = soft * (d_probs - jnp.sum(d_probs * soft, axis=-1, keepdims=True))
    d_scores = d_scores.astype(jnp.bfloat16)
    query_input_grad = (
        jnp.einsum("shqk,skhe->sqhe", d_scores, key_heads, preferred_element_type=jnp.float32)
        * 0.125
    )
    query_input_grad = query_input_grad.reshape(slot_count, query_rows, inner_width).astype(
        jnp.bfloat16
    )
    d_keys = (
        jnp.einsum("shqk,sqhe->skhe", d_scores, query_heads, preferred_element_type=jnp.float32)
        * 0.125
    )
    d_pairs = jnp.concatenate(
        [
            d_keys.reshape(slot_count, key_rows, inner_width),
            d_values.reshape(slot_count, key_rows, inner_width),
        ],
        axis=-1,
    )
    own_pairs = lax.psum_scatter(
        d_pairs.astype(jnp.bfloat16), "lat", scatter_dimension=1, tiled=True
    )
    key_value_term = jnp.einsum(
        "skd,ske->de", joined, own_pairs, preferred_element_type=jnp.float32
    )
    d_joined = jnp.einsum("ske,de->skd", own_pairs, key_value_w, preferred_element_type=jnp.float32)
    normed_latent_rows = joined[:, patch_rows:]
    query_contribution = jnp.einsum(
        "jmk,jmw->kw", normed_latent_rows, query_input_grad, preferred_element_type=jnp.float32
    )
    d_latent_norm = d_joined[:, patch_rows:] + jnp.einsum(
        "nra,xa->nrx", query_input_grad, query_projection_weight, preferred_element_type=jnp.float32
    )
    _, media_pull = jax.vjp(norm_rows, media_float, gain_rows[0], shift_rows[0])
    d_media, gain_media, shift_media = media_pull(d_joined[:, :patch_rows])
    _, latent_pull = jax.vjp(norm_rows, latent_rows, gain_rows[1], shift_rows[1])
    d_latent, gain_latent, shift_latent = latent_pull(d_latent_norm)
    d_rows = d_latent + d_after
    gain_terms = jnp.stack([gain_media, gain_latent, gain_feed])
    shift_terms = jnp.stack([shift_media, shift_latent, shift_feed])
    attention_summed = (
        lax.psum_scatter(query_contribution, ("img", "lat"), scatter_dimension=0, tiled=True),
        lax.psum_scatter(key_value_term, ("img", "lat"), scatter_dimension=0, tiled=True),
        lax.psum_scatter(output_term, ("img", "lat"), scatter_dimension=0, tiled=True),
        lax.psum_scatter(gain_terms, ("img", "lat"), scatter_dimension=1, tiled=True),
        lax.psum_scatter(shift_terms, ("img", "lat"), scatter_dimension=1, tiled=True),
    )
    summed = (
        attention_summed[0],
        attention_summed[1],
        attention_summed[2],
        up_summed,
        down_summed,
        attention_summed[3],
        attention_summed[4],
    )
    return (d_rows, d_media, summed)


def per_device(
    media_tokens,
    image_counts,
    latent_init,
    cotangent,
    query_weight,
    key_value_weight,
    output_weight,
    up_weight,
    down_weight,
    norm_gain,
    norm_shift,
):
    slot_count = media_tokens.shape[0]
    model_width = media_tokens.shape[2]
    latent_count = latent_init.shape[0]
    position = jnp.arange(slot_count) % MEDIA
    per_slot = jnp.repeat(image_counts, MEDIA)
    valid_mask = (position < per_slot).astype(jnp.float32)[:, None, None]
    media_float = media_tokens.astype(jnp.float32)
    latent_rows = jnp.broadcast_to(
        latent_init.astype(jnp.float32), (slot_count, latent_count, model_width)
    )
    stored_layers = []
    for level_index in range(LAYERS):
        current = (
            lax.all_gather(query_weight[level_index], ("img", "lat"), axis=0, tiled=True),
            lax.all_gather(key_value_weight[level_index], ("img", "lat"), axis=0, tiled=True),
            lax.all_gather(output_weight[level_index], ("img", "lat"), axis=0, tiled=True),
            lax.all_gather(up_weight[level_index], ("img", "lat"), axis=0, tiled=True),
            lax.all_gather(down_weight[level_index], ("img", "lat"), axis=0, tiled=True),
            lax.all_gather(norm_gain[level_index], ("img", "lat"), axis=1, tiled=True),
            lax.all_gather(norm_shift[level_index], ("img", "lat"), axis=1, tiled=True),
        )
        latent_rows, stored = layer_forward(latent_rows, media_float, current)
        stored_layers.append(stored)
    resampled = latent_rows * valid_mask
    upstream = cotangent.astype(jnp.float32) * valid_mask
    media_grad = jnp.zeros(media_float.shape, jnp.float32)
    layer_grads = [None] * LAYERS
    for level_index in reversed(range(LAYERS)):
        current = (
            lax.all_gather(query_weight[level_index], ("img", "lat"), axis=0, tiled=True),
            lax.all_gather(key_value_weight[level_index], ("img", "lat"), axis=0, tiled=True),
            lax.all_gather(output_weight[level_index], ("img", "lat"), axis=0, tiled=True),
            lax.all_gather(up_weight[level_index], ("img", "lat"), axis=0, tiled=True),
            lax.all_gather(down_weight[level_index], ("img", "lat"), axis=0, tiled=True),
            lax.all_gather(norm_gain[level_index], ("img", "lat"), axis=1, tiled=True),
            lax.all_gather(norm_shift[level_index], ("img", "lat"), axis=1, tiled=True),
        )
        upstream, d_media, summed = layer_backward(
            upstream, media_float, current, stored_layers[level_index]
        )
        media_grad = media_grad + d_media
        layer_grads[level_index] = summed
    latent_grad = lax.psum(jnp.sum(upstream, axis=0), "img")
    query_grad = jnp.stack([entry[0] for entry in layer_grads])
    key_value_grad = jnp.stack([entry[1] for entry in layer_grads])
    output_grad = jnp.stack([entry[2] for entry in layer_grads])
    up_grad = jnp.stack([entry[3] for entry in layer_grads])
    down_grad = jnp.stack([entry[4] for entry in layer_grads])
    gain_grad = jnp.stack([entry[5] for entry in layer_grads])
    shift_grad = jnp.stack([entry[6] for entry in layer_grads])
    return (
        resampled,
        media_grad,
        latent_grad,
        query_grad,
        key_value_grad,
        output_grad,
        up_grad,
        down_grad,
        gain_grad,
        shift_grad,
    )


def solution(mesh):
    in_specs = (
        P("img", "lat", None),
        P("img"),
        P("lat", None),
        P("img", "lat", None),
        P(None, ("img", "lat"), None),
        P(None, ("img", "lat"), None),
        P(None, ("img", "lat"), None),
        P(None, ("img", "lat"), None),
        P(None, ("img", "lat"), None),
        P(None, None, ("img", "lat")),
        P(None, None, ("img", "lat")),
    )
    out_specs = (
        P("img", "lat", None),
        P("img", "lat", None),
        P("lat", None),
        P(None, ("img", "lat"), None),
        P(None, ("img", "lat"), None),
        P(None, ("img", "lat"), None),
        P(None, ("img", "lat"), None),
        P(None, ("img", "lat"), None),
        P(None, None, ("img", "lat")),
        P(None, None, ("img", "lat")),
    )
    return jax.shard_map(
        per_device, mesh=mesh, in_specs=in_specs, out_specs=out_specs, check_vma=False
    )
```

profile of v0, /device:TPU:0, one launch (start us, length us, event | category | flops | bytes accessed | tf_op | source)
XLA Modules:
  0.0 3144.0 jit_solution(1778448005791190443)
XLA Ops:
  16.3 44.9 %all-gather = bf16[1,3,1024]{1,0,2:T(2,128)(2,1)S(1)} all-gather(bf16[1,3,32]{1,0,2:T(2,128)(2,1)S(1)} %copy.125), channel_id=2, replica_groups=mesh['img'=16,'lat'=2] {'img','lat'}, dimensions={2}, use_global_device_ids=true | all-gather | bytes 6336 | tf_op jit(solution)/shard_map/all_gather | solution.py:256
  61.7 10.4 slice_reduce_fusion.9
  72.1 38.3 %all-gather.1 = bf16[1,3,1024]{1,0,2:T(2,128)(2,1)S(1)} all-gather(bf16[1,3,32]{1,0,2:T(2,128)(2,1)S(1)} %copy.126), channel_id=3, replica_groups=mesh['img'=16,'lat'=2] {'img','lat'}, dimensions={2}, use_global_device_ids=true | all-gather | bytes 6336 | tf_op jit(solution)/shard_map/all_gather | solution.py:257
  110.9 39.6 %all-gather.7 = bf16[1,3,1024]{1,0,2:T(2,128)(2,1)S(1)} all-gather(bf16[1,3,32]{1,0,2:T(2,128)(2,1)S(1)} %copy.127), channel_id=9, replica_groups=mesh['img'=16,'lat'=2] {'img','lat'}, dimensions={2}, use_global_device_ids=true | all-gather | bytes 6336 | tf_op jit(solution)/shard_map/all_gather | solution.py:256
  151.1 38.5 %all-gather.8 = bf16[1,3,1024]{1,0,2:T(2,128)(2,1)S(1)} all-gather(bf16[1,3,32]{1,0,2:T(2,128)(2,1)S(1)} %copy.128), channel_id=10, replica_groups=mesh['img'=16,'lat'=2] {'img','lat'}, dimensions={2}, use_global_device_ids=true | all-gather | bytes 6336 | tf_op jit(solution)/shard_map/all_gather | solution.py:257
  190.4 10.4 slice_reduce_fusion.8
  201.6 10.6 slice_reduce_fusion.3
  212.2 10.6 slice_reduce_fusion.2
  255.9 41.4 %all-gather.35.cloned.1.call-done = bf16[1,512,1024]{2,1,0:T(8,128)(2,1)} async-done(((bf16[1,16,1024]{2,1,0:T(8,128)(2,1)}), bf16[1,512,1024]{2,1,0:T(8,128)(2,1)}) %all-gather.35.cloned.1.call-update) | async-done | bytes 1048592 | tf_op jit(solution)/shard_map/all_gather | solution.py:253
  300.2 76.5 %all-gather.37.cloned.1.call-done = bf16[1,1024,4096]{2,1,0:T(8,128)(2,1)} async-done(((bf16[1,32,4096]{2,1,0:T(8,128)(2,1)}), bf16[1,1024,4096]{2,1,0:T(8,128)(2,1)}) %all-gather.37.cloned.1.call-update) | async-done | bytes 8388624 | tf_op jit(solution)/shard_map/all_gather | solution.py:254
  391.0 64.7 %all-gather.39.cloned.1.call-done = bf16[1,4096,1024]{2,1,0:T(8,128)(2,1)} async-done(((bf16[1,128,1024]{2,1,0:T(8,128)(2,1)}), bf16[1,4096,1024]{2,1,0:T(8,128)(2,1)}) %all-gather.39.cloned.1.call-update) | async-done | bytes 8388624 | tf_op jit(solution)/shard_map/all_gather | solution.py:255
  462.9 51.1 %all-gather.41.cloned.1.call-done = bf16[1,1024,1024]{2,1,0:T(8,128)(2,1)} async-done(((bf16[1,32,1024]{2,1,0:T(8,128)(2,1)}), bf16[1,1024,1024]{2,1,0:T(8,128)(2,1)}) %all-gather.41.cloned.1.call-update) | async-done | bytes 2097168 | tf_op jit(solution)/shard_map/all_gather | solution.py:252
  522.8 47.2 %all-gather.43.cloned.1.call-done = bf16[1,1024,512]{2,1,0:T(8,128)(2,1)} async-done(((bf16[1,32,512]{2,1,0:T(8,128)(2,1)}), bf16[1,1024,512]{2,1,0:T(8,128)(2,1)}) %all-gather.43.cloned.1.call-update) | async-done | bytes 1048592 | tf_op jit(solution)/shard_map/all_gather | solution.py:251
  600.8 40.1 %all-gather.45.cloned.1.call-done = bf16[1,512,1024]{2,1,0:T(8,128)(2,1)} async-done(((bf16[1,16,1024]{2,1,0:T(8,128)(2,1)}), bf16[1,512,1024]{2,1,0:T(8,128)(2,1)}) %all-gather.45.cloned.1.call-update) | async-done | bytes 1048592 | tf_op jit(solution)/shard_map/all_gather | solution.py:253
  645.1 75.3 %all-gather.47.cloned.1.call-done = bf16[1,1024,4096]{2,1,0:T(8,128)(2,1)} async-done(((bf16[1,32,4096]{2,1,0:T(8,128)(2,1)}), bf16[1,1024,4096]{2,1,0:T(8,128)(2,1)}) %all-gather.47.cloned.1.call-update) | async-done | bytes 8388624 | tf_op jit(solution)/shard_map/all_gather | solution.py:254
  735.1 63.7 %all-gather.49.cloned.1.call-done = bf16[1,4096,1024]{2,1,0:T(8,128)(2,1)} async-done(((bf16[1,128,1024]{2,1,0:T(8,128)(2,1)}), bf16[1,4096,1024]{2,1,0:T(8,128)(2,1)}) %all-gather.49.cloned.1.call-update) | async-done | bytes 8388624 | tf_op jit(solution)/shard_map/all_gather | solution.py:255
  951.1 9.5 convolution_bitcast_fusion.3
  988.6 64.9 %reduce-scatter.39.cloned.1.call-done = f32[16,1024]{1,0:T(8,128)} async-done(((f32[512,1024]{1,0:T(8,128)}), f32[16,1024]{1,0:T(8,128)}) %reduce-scatter.39.cloned.1.call-update) | async-done | bytes 65552 | tf_op jit(solution)/shard_map/reduce_scatter | solution.py:209
  1053.6 136.2 %reduce-scatter.37.cloned.1.call-done = f32[16,1024]{1,0:T(8,128)} async-done(((f32[512,1024]{1,0:T(8,128)}), f32[16,1024]{1,0:T(8,128)}) %reduce-scatter.37.cloned.1.call-update) | async-done | bytes 65552 | tf_op jit(solution)/shard_map/reduce_scatter | solution.py:209
  1191.3 135.1 %reduce-scatter.31.cloned.1.call-done = f32[32,512]{1,0:T(8,128)} async-done(((f32[1024,512]{1,0:T(8,128)}), f32[32,512]{1,0:T(8,128)}) %reduce-scatter.31.cloned.1.call-update) | async-done | bytes 65552 | tf_op jit(solution)/shard_map/reduce_scatter | solution.py:207
  1326.4 136.1 %reduce-scatter.29.cloned.1.call-done = f32[32,512]{1,0:T(8,128)} async-done(((f32[1024,512]{1,0:T(8,128)}), f32[32,512]{1,0:T(8,128)}) %reduce-scatter.29.cloned.1.call-update) | async-done | bytes 65552 | tf_op jit(solution)/shard_map/reduce_scatter | solution.py:207
  1468.5 128.0 %reduce-scatter.49.cloned.1.call-done = f32[32,3]{1,0:T(8,128)} async-done(((f32[1024,3]{1,0:T(8,128)}), f32[32,3]{1,0:T(8,128)}) %reduce-scatter.49.cloned.1.call-update) | async-done | bytes 400
  1597.2 132.9 %reduce-scatter.53.cloned.1.call-done = f32[32,3]{1,0:T(8,128)} async-done(((f32[1024,3]{1,0:T(8,128)}), f32[32,3]{1,0:T(8,128)}) %reduce-scatter.53.cloned.1.call-update) | async-done | bytes 400
  1731.0 133.2 %reduce-scatter.55.cloned.1.call-done = f32[32,3]{1,0:T(8,128)} async-done(((f32[1024,3]{1,0:T(8,128)}), f32[32,3]{1,0:T(8,128)}) %reduce-scatter.55.cloned.1.call-update) | async-done | bytes 400
  1865.6 133.1 %reduce-scatter.51.cloned.1.call-done = f32[32,3]{1,0:T(8,128)} async-done(((f32[1024,3]{1,0:T(8,128)}), f32[32,3]{1,0:T(8,128)}) %reduce-scatter.51.cloned.1.call-update) | async-done | bytes 400
  2000.1 139.9 %reduce-scatter.35.cloned.1.call-done = f32[32,1024]{1,0:T(8,128)} async-done(((f32[1024,1024]{1,0:T(8,128)}), f32[32,1024]{1,0:T(8,128)}) %reduce-scatter.35.cloned.1.call-update) | async-done | bytes 131088 | tf_op jit(solution)/shard_map/reduce_scatter | solution.py:208
  2140.0 140.9 %reduce-scatter.33.cloned.1.call-done = f32[32,1024]{1,0:T(8,128)} async-done(((f32[1024,1024]{1,0:T(8,128)}), f32[32,1024]{1,0:T(8,128)}) %reduce-scatter.33.cloned.1.call-update) | async-done | bytes 131088 | tf_op jit(solution)/shard_map/reduce_scatter | solution.py:208
  2282.6 179.4 %reduce-scatter.43.cloned.1.call-done = f32[32,4096]{1,0:T(8,128)} async-done(((f32[1024,4096]{1,0:T(8,128)}), f32[32,4096]{1,0:T(8,128)}) %reduce-scatter.43.cloned.1.call-update) | async-done | bytes 524304 | tf_op jit(solution)/shard_map/reduce_scatter | solution.py:137
  2462.0 186.8 %reduce-scatter.41.cloned.1.call-done = f32[32,4096]{1,0:T(8,128)} async-done(((f32[1024,4096]{1,0:T(8,128)}), f32[32,4096]{1,0:T(8,128)}) %reduce-scatter.41.cloned.1.call-update) | async-done | bytes 524304 | tf_op jit(solution)/shard_map/reduce_scatter | solution.py:137
  2651.0 184.5 %reduce-scatter.47.cloned.1.call-done = f32[128,1024]{1,0:T(8,128)} async-done(((f32[4096,1024]{1,0:T(8,128)}), f32[128,1024]{1,0:T(8,128)}) %reduce-scatter.47.cloned.1.call-update) | async-done | bytes 524304 | tf_op jit(solution)/shard_map/reduce_scatter | solution.py:126
  2835.6 186.9 %reduce-scatter.45.cloned.1.call-done = f32[128,1024]{1,0:T(8,128)} async-done(((f32[4096,1024]{1,0:T(8,128)}), f32[128,1024]{1,0:T(8,128)}) %reduce-scatter.45.cloned.1.call-update) | async-done | bytes 524304 | tf_op jit(solution)/shard_map/reduce_scatter | solution.py:126
  3024.8 110.9 %all-reduce.2.cloned.1.call-done = f32[32,1024]{1,0:T(8,128)} async-done(((f32[32,1024]{1,0:T(8,128)}), f32[32,1024]{1,0:T(8,128)}) %all-reduce.2.cloned.1.call-update) | async-done | bytes 131088 | tf_op jit(solution)/shard_map/psum | solution.py:280
  (402 shorter events, 325.9 us)
Async XLA Ops:
  7.2 217.5 %all-gather.31.cloned.1.call-start = ((), (), s32[]{:S(2)}) async-start(), calls=%async_computation.31 | async-start | bytes 2162688 | tf_op jit(solution)/shard_map/all_gather | solution.py:252
  8.9 225.1 %all-gather.33.cloned.1.call-start = ((), (), s32[]{:S(2)}) async-start(), calls=%async_computation.32 | async-start | bytes 1081344 | tf_op jit(solution)/shard_map/all_gather | solution.py:251
  10.4 229.5 %all-gather.27.cloned.1.call-start = ((), (), s32[]{:S(2)}) async-start(), calls=%async_computation.16 | async-start | bytes 4915200 | tf_op jit(solution)/shard_map/all_gather | solution.py:46
  12.2 221.8 %copy-start.76 = (f32[32]{0:T(128)}, f32[32]{0:T(128)S(1)}, u32[]{:S(2)}) copy-start(f32[32]{0:T(128)S(1)} %broadcast_multiply_fusion.4) | copy-start | bytes 388
  72.1 304.6 %copy-start.67 = (f32[1024]{0:T(1024)}, f32[1024]{0:T(1024)S(1)}, u32[]{:S(2)}) copy-start(f32[1024]{0:T(1024)S(1)} %get-tuple-element.85) | copy-start | bytes 12292
  229.9 67.4 %all-gather.35.cloned.1.call-start = ((), (), s32[]{:S(2)}) async-start(), calls=%async_computation.33 | async-start | bytes 1081344 | tf_op jit(solution)/shard_map/all_gather | solution.py:253
  230.6 146.1 %all-gather.37.cloned.1.call-start = ((), (), s32[]{:S(2)}) async-start(), calls=%async_computation.34 | async-start | bytes 8650752 | tf_op jit(solution)/shard_map/all_gather | solution.py:254
  231.5 224.2 %all-gather.39.cloned.1.call-start = ((), (), s32[]{:S(2)}) async-start(), calls=%async_computation.35 | async-start | bytes 8650752 | tf_op jit(solution)/shard_map/all_gather | solution.py:255
  232.4 281.6 %all-gather.41.cloned.1.call-start = ((), (), s32[]{:S(2)}) async-start(), calls=%async_computation.36 | async-start | bytes 2162688 | tf_op jit(solution)/shard_map/all_gather | solution.py:252
  233.2 336.7 %all-gather.43.cloned.1.call-start = ((), (), s32[]{:S(2)}) async-start(), calls=%async_computation.37 | async-start | bytes 1081344 | tf_op jit(solution)/shard_map/all_gather | solution.py:251
  234.0 348.9 %all-gather.29.cloned.1.call-start = ((), (), s32[]{:S(2)}) async-start(), calls=%async_computation.17 | async-start | bytes 4915200 | tf_op jit(solution)/shard_map/all_gather | solution.py:46
  253.2 123.5 %copy-start.80 = (f32[1024]{0:T(1024)S(1)}, f32[1024]{0:T(1024)}, u32[]{:S(2)}) copy-start(f32[1024]{0:T(1024)} %get-tuple-element.88) | copy-start | bytes 12292
  519.2 121.7 %all-gather.45.cloned.1.call-start = ((), (), s32[]{:S(2)}) async-start(), calls=%async_computation.38 | async-start | bytes 1081344 | tf_op jit(solution)/shard_map/all_gather | solution.py:253
  519.8 200.6 %all-gather.47.cloned.1.call-start = ((), (), s32[]{:S(2)}) async-start(), calls=%async_computation.39 | async-start | bytes 8650752 | tf_op jit(solution)/shard_map/all_gather | solution.py:254
  520.6 278.2 %all-gather.49.cloned.1.call-start = ((), (), s32[]{:S(2)}) async-start(), calls=%async_computation.40 | async-start | bytes 8650752 | tf_op jit(solution)/shard_map/all_gather | solution.py:255
  521.1 333.6 %reduce-scatter.25.cloned.1.call-start = ((), (), s32[]{:S(2)}) async-start(), calls=%async_computation.18 | async-start | bytes 4915200 | tf_op jit(solution)/shard_map/reduce_scatter | solution.py:185
  844.8 67.2 %reduce-scatter.27.cloned.1.call-start = ((), (), s32[]{:S(2)}) async-start(), calls=%async_computation.19 | async-start | bytes 4915200 | tf_op jit(solution)/shard_map/reduce_scatter | solution.py:185
  899.4 154.2 %reduce-scatter.39.cloned.1.call-start = ((), (), s32[]{:S(2)}) async-start(), calls=%async_computation.26 | async-start | bytes 2162688 | tf_op jit(solution)/shard_map/reduce_scatter | solution.py:209
  902.2 287.5 %reduce-scatter.37.cloned.1.call-start = ((), (), s32[]{:S(2)}) async-start(), calls=%async_computation.25 | async-start | bytes 2162688 | tf_op jit(solution)/shard_map/reduce_scatter | solution.py:209
  904.1 422.3 %reduce-scatter.31.cloned.1.call-start = ((), (), s32[]{:S(2)}) async-start(), calls=%async_computation.22 | async-start | bytes 2162688 | tf_op jit(solution)/shard_map/reduce_scatter | solution.py:207
  907.2 555.3 %reduce-scatter.29.cloned.1.call-start = ((), (), s32[]{:S(2)}) async-start(), calls=%async_computation.21 | async-start | bytes 2162688 | tf_op jit(solution)/shard_map/reduce_scatter | solution.py:207
  911.9 684.6 %reduce-scatter.49.cloned.1.call-start = ((), (), s32[]{:S(2)}) async-start(), calls=%async_computation.41 | async-start | bytes 540672
  923.6 806.6 %reduce-scatter.53.cloned.1.call-start = ((), (), s32[]{:S(2)}) async-start(), calls=%async_computation.43 | async-start | bytes 540672
  924.8 939.4 %reduce-scatter.55.cloned.1.call-start = ((), (), s32[]{:S(2)}) async-start(), calls=%async_computation.44 | async-start | bytes 540672
  925.9 1072.8 %reduce-scatter.51.cloned.1.call-start = ((), (), s32[]{:S(2)}) async-start(), calls=%async_computation.42 | async-start | bytes 540672
  927.1 1212.9 %reduce-scatter.35.cloned.1.call-start = ((), (), s32[]{:S(2)}) async-start(), calls=%async_computation.24 | async-start | bytes 4325376 | tf_op jit(solution)/shard_map/reduce_scatter | solution.py:208
  933.1 1347.8 %reduce-scatter.33.cloned.1.call-start = ((), (), s32[]{:S(2)}) async-start(), calls=%async_computation.23 | async-start | bytes 4325376 | tf_op jit(solution)/shard_map/reduce_scatter | solution.py:208
  940.3 1521.7 %reduce-scatter.43.cloned.1.call-start = ((), (), s32[]{:S(2)}) async-start(), calls=%async_computation.28 | async-start | bytes 17301504 | tf_op jit(solution)/shard_map/reduce_scatter | solution.py:137
  950.0 1698.8 %reduce-scatter.41.cloned.1.call-start = ((), (), s32[]{:S(2)}) async-start(), calls=%async_computation.27 | async-start | bytes 17301504 | tf_op jit(solution)/shard_map/reduce_scatter | solution.py:137
  960.6 1874.9 %reduce-scatter.47.cloned.1.call-start = ((), (), s32[]{:S(2)}) async-start(), calls=%async_computation.30 | async-start | bytes 17301504 | tf_op jit(solution)/shard_map/reduce_scatter | solution.py:126
  971.1 2051.4 %reduce-scatter.45.cloned.1.call-start = ((), (), s32[]{:S(2)}) async-start(), calls=%async_computation.29 | async-start | bytes 17301504 | tf_op jit(solution)/shard_map/reduce_scatter | solution.py:126
  981.6 2154.1 %all-reduce.2.cloned.1.call-start = ((), (), s32[]{:S(2)}) async-start(), calls=%async_computation.20 | async-start | bytes 262144 | tf_op jit(solution)/shard_map/psum | solution.py:280
  (89 other events, 708.5 us)
Sparse Core Ops, SparseCore 0:
  11.4 59.6 all-gather.30
  74.5 52.9 all-gather.32
  230.0 9.7 all-gather.26
  242.6 54.7 all-gather.34
  300.7 76.0 all-gather.36
  380.0 75.6 all-gather.38
  459.2 54.8 all-gather.40
  517.5 52.4 all-gather.42
  571.5 11.2 all-gather.28
  586.1 54.7 all-gather.44
  644.4 76.0 all-gather.46
  723.1 75.6 all-gather.48
  844.9 9.7 reduce-scatter.24
  899.5 12.4 reduce-scatter.26
  914.1 139.4 reduce-scatter.38
  1055.7 134.0 reduce-scatter.36
  1192.4 133.9 reduce-scatter.30
  1328.5 133.9 reduce-scatter.28
  1464.8 131.6 reduce-scatter.48
  1598.5 131.6 reduce-scatter.52
  1732.4 131.7 reduce-scatter.54
  1867.0 131.6 reduce-scatter.50
  2001.0 138.9 reduce-scatter.34
  2142.1 138.7 reduce-scatter.32
  2283.2 178.7 reduce-scatter.42
  2464.1 184.6 reduce-scatter.40
  2650.9 184.5 reduce-scatter.46
  2837.9 184.5 reduce-scatter.44
  3028.5 107.0 all-reduce.1
where the time goes:
time: 3150 us; the launch traced here: 3140 us
  waiting for transfers between devices  2610 us (83%)
  matrix products  162 us (5%)
  blocking collectives  161 us (5%)
  local copies, waits for them, and re-layouts  134 us (4%)
  other arithmetic  59.8 us (2%)
    unnamed x33, waiting for transfers between devices  531 us
    reduce_scatter x2, waiting for transfers between devices, layer_backward(): lax.psum_scatter(down_contribution, ('img', 'lat'), scatter_dimension=0,...  371 us
    reduce_scatter x2, waiting for transfers between devices, layer_backward(): lax.psum_scatter(up_contribution, ('img', 'lat'), scatter_dimension=0, ti...  366 us
    reduce_scatter x2, waiting for transfers between devices, layer_backward(): lax.psum_scatter(key_value_term, ('img', 'lat'), scatter_dimension=0, til...  281 us
    reduce_scatter x2, waiting for transfers between devices, layer_backward(): lax.psum_scatter(query_contribution, ('img', 'lat'), scatter_dimension=0,...  271 us
    reduce_scatter x2, waiting for transfers between devices, layer_backward(): lax.psum_scatter(output_term, ('img', 'lat'), scatter_dimension=0, tiled=...  201 us
    all_gather x2, waiting for transfers between devices, per_device(): lax.all_gather(up_weight[level_index], ('img', 'lat'), axis=0, tiled=True)  152 us
    all_gather x2, waiting for transfers between devices, per_device(): lax.all_gather(down_weight[level_index], ('img', 'lat'), axis=0, tiled=True)  128 us
  transfers between devices with their start and end apart: 29, of which 27 were waited for; matrix products, arithmetic and copies ran while one was open for 8% of the time, Pallas kernels for 0%

commit v1 on v0

v1 whole, which is shorter than its diff:
```python
import jax
import jax.numpy as jnp
from jax import lax
from jax.sharding import PartitionSpec as P

HEAD = 64
MEDIA = 5
LAYERS = 2
F32 = jnp.float32
BF16 = jnp.bfloat16


class Bit:
    def __init__(self, axis, size, place, rank):
        self.rank = rank
        self.axis = axis
        self.mask = 1 << place
        self.pairs = [(source, source ^ self.mask) for source in range(size)]

    def mine(self):
        return (lax.axis_index(self.axis) // self.mask) % 2

    def swap(self, array):
        return lax.ppermute(array, self.axis, self.pairs)


class Layout:
    def __init__(self, img, lat):
        lat_bits = [Bit("lat", lat, k, k) for k in range(lat.bit_length() - 1)]
        img_bits = [Bit("img", img, k, k + len(lat_bits)) for k in range(img.bit_length() - 1)]
        self.devices = img * lat
        self.lat = lat_bits
        self.img = img_bits
        self.first, self.second = img_bits[0], img_bits[1]
        self.tensor_img = img_bits[2]
        self.far = list(reversed(img_bits[3:]))
        self.tensor = [self.tensor_img] + list(reversed(lat_bits))
        self.split = 2 ** len(self.tensor)


def join(array, order, have):
    have = list(have)
    for bit in order:
        other = bit.swap(array)
        low = bit.mine() == 0
        place = sum(1 for held in have if held.rank > bit.rank)
        array = jnp.stack([jnp.where(low, array, other), jnp.where(low, other, array)], axis=place)
        have.insert(place, bit)
    return array, have


def part(array, bit, place, own):
    index = bit.mine() if own else 1 - bit.mine()
    return lax.dynamic_index_in_dim(array, index, place, keepdims=False)


def shed(array, order, have):
    have = list(have)
    for bit in order:
        place = have.index(bit)
        other = bit.swap(part(array, bit, place, False).astype(BF16))
        array = part(array, bit, place, True).astype(F32) + other.astype(F32)
        have.pop(place)
    return array, have


def all_sum(array, order):
    for bit in order:
        array = array + bit.swap(array)
    return array


def norm_rows(inputs, scale_row, shift_row):
    average = jnp.mean(inputs, axis=-1, keepdims=True)
    centered = inputs - average
    variance = jnp.mean(centered * centered, axis=-1, keepdims=True)
    return centered * lax.rsqrt(variance + 1e-05) * scale_row + shift_row


def mm(a, b):
    return lax.dot_general(a, b, (((1,), (0,)), ((), ())), preferred_element_type=F32)


def mm_nt(a, b):
    return lax.dot_general(a, b, (((1,), (1,)), ((), ())), preferred_element_type=F32)


def mm_tn(a, b):
    return lax.dot_general(a, b, (((0,), (0,)), ((), ())), preferred_element_type=F32)


class Weights:
    pass


def gather_attention(lay, kv_shard, out_shard, query_shard, extra):
    rows = kv_shard.shape[0]
    half = rows // 2
    query_pack = jnp.concatenate([query_shard[:half], query_shard[half:]], axis=1)
    parts = [kv_shard, out_shard, query_pack]
    if extra is not None:
        parts.append(extra)
    packed = jnp.concatenate(parts, axis=0)
    packed, have = join(packed, lay.far + [lay.tensor_img], [])
    left = packed[..., :rows, :]
    right = packed[..., rows:, :]
    left, left_have = join(left, [lay.first, lay.second], have)
    right, right_have = join(right, [lay.second, lay.first], have)
    left, _ = join(left, lay.lat, left_have)
    right, _ = join(right, lay.lat, right_have)
    width = kv_shard.shape[1]
    key_value = left.reshape(-1, width)
    right = right.reshape((lay.devices,) + right.shape[-2:])
    out_rows = out_shard.shape[0]
    output = right[:, :out_rows].reshape(-1, width)
    pack = right[:, out_rows : out_rows + half]
    query = jnp.concatenate([pack[..., : width // 2], pack[..., width // 2 :]], axis=1)
    query = query.reshape(-1, width // 2)
    if extra is None:
        return key_value, output, query, None
    norms = jnp.sum(right[:, out_rows + half :].astype(F32), axis=0)
    return key_value, output, query, norms


def feed_columns(lay, array, forward):
    width = array.shape[-1] // lay.devices if forward else None
    ranks = [bit.rank for bit in lay.tensor]
    owner = []
    for device in range(lay.devices):
        value = 0
        for rank in ranks:
            value = value * 2 + (device >> rank) % 2
        owner.append(value)
    if forward:
        blocks = [array[..., d * width : (d + 1) * width] for d in range(lay.devices)]
        sets = [
            jnp.concatenate([blocks[d] for d in range(lay.devices) if owner[d] == s], axis=-1)
            for s in range(lay.split)
        ]
        return jnp.stack(sets)
    width = array.shape[-1] * lay.split // lay.devices
    seen = [0] * lay.split
    blocks = []
    for device in range(lay.devices):
        s = owner[device]
        blocks.append(array[s, :, seen[s] * width : (seen[s] + 1) * width])
        seen[s] += 1
    return jnp.concatenate(blocks, axis=-1)


def exchange(array, bit, place):
    other = bit.swap(part(array, bit, place, False))
    own = part(array, bit, place, True)
    low = bit.mine() == 0
    return jnp.stack([jnp.where(low, own, other), jnp.where(low, other, own)], axis=place)


def gather_feed(lay, up_shard, down_shard):
    rows = up_shard.shape[0]
    width = down_shard.shape[1]
    columns = up_shard.shape[1] // lay.split
    up = feed_columns(lay, up_shard, True)
    up = up.reshape((2,) * len(lay.tensor) + (rows, columns))
    for place in reversed(range(len(lay.tensor))):
        up = exchange(up, lay.tensor[place], place)
    up, have = join(up, lay.far, lay.tensor)
    down, down_have = join(down_shard, lay.far, [])
    up, _ = join(up, [lay.first, lay.second], have)
    down, _ = join(down, [lay.second, lay.first], down_have)
    return up.reshape(-1, columns), down.reshape(-1, width)


def reduce_feed(lay, up_term, down_term, rows):
    columns = up_term.shape[1]
    width = down_term.shape[1]
    every = list(reversed(lay.lat + lay.img))
    have = [bit for bit in every]
    up = up_term.reshape((2,) * len(have) + (rows, columns))
    up, have = shed(up, [lay.second, lay.first], have)
    rest = [bit for bit in every if bit not in lay.tensor]
    down = down_term.reshape((2,) * len(rest) + (-1, width))
    down, rest = shed(down, [lay.first, lay.second], rest)
    far = list(reversed(lay.far))
    up, have = shed(up, far, have)
    down, rest = shed(down, far, rest)
    up = up.astype(BF16)
    for place in range(len(lay.tensor)):
        up = exchange(up, lay.tensor[place], place)
    up = feed_columns(lay, up.reshape(lay.split, rows, columns), False)
    return up.astype(F32), down


def reduce_attention(lay, key_value_term, output_term, query_term):
    width = key_value_term.shape[1]
    every = list(reversed(lay.lat + lay.img))
    rows = key_value_term.shape[0] // lay.devices
    half = rows // 2
    out_rows = output_term.shape[0] // lay.devices
    left = key_value_term.astype(BF16).reshape((2,) * len(every) + (rows, width))
    query = query_term.astype(BF16).reshape(lay.devices, 2, half, width // 2)
    query = jnp.concatenate([query[:, 0], query[:, 1]], axis=-1)
    right = jnp.concatenate(
        [output_term.astype(BF16).reshape(lay.devices, out_rows, width), query], axis=1
    )
    right = right.reshape((2,) * len(every) + (out_rows + half, width))
    left, left_have = shed(left, lay.lat, every)
    right, right_have = shed(right, lay.lat, every)
    left, left_have = shed(left, [lay.second, lay.first], left_have)
    right, right_have = shed(right, [lay.first, lay.second], right_have)
    packed = jnp.concatenate([left, right], axis=-2)
    packed, _ = shed(packed, [lay.tensor_img] + list(reversed(lay.far)), left_have)
    output = packed[rows : rows + out_rows]
    pack = packed[rows + out_rows :]
    query = jnp.concatenate([pack[:, : width // 2], pack[:, width // 2 :]], axis=0)
    return packed[:rows], output, query


def gather_rows(lay, rows):
    joined, _ = join(rows, lay.tensor, [])
    return joined.reshape(-1, rows.shape[-1])


def return_rows(lay, rows):
    array = rows.reshape((2,) * len(lay.tensor) + (-1, rows.shape[-1]))
    array, _ = shed(array, list(reversed(lay.tensor)), lay.tensor)
    return array


def layer_forward(lay, latent_rows, media_float, current):
    query_w, key_value_w, output_w, up_w, down_w, gain_rows, shift_rows = current
    inner_width = query_w.shape[1]
    head_count = inner_width // HEAD
    slot_count, query_rows, model = latent_rows.shape
    media_norm = norm_rows(media_float, gain_rows[0], shift_rows[0]).astype(BF16)
    normed_latent_rows = norm_rows(latent_rows, gain_rows[1], shift_rows[1]).astype(BF16)
    query = mm(normed_latent_rows.reshape(-1, model), query_w).astype(BF16)
    joined = jnp.concatenate([media_norm, normed_latent_rows], axis=1)
    own_pairs = mm(joined.reshape(-1, model), key_value_w).astype(BF16)
    own_pairs = own_pairs.reshape(slot_count, -1, 2 * inner_width)
    key_value, _ = join(own_pairs, lay.lat, [])
    key_value = jnp.concatenate([key_value[k] for k in range(key_value.shape[0])], axis=1)
    key_rows = key_value.shape[1]
    query_heads = query.reshape(slot_count, query_rows, head_count, HEAD)
    key_heads = key_value[..., :inner_width].reshape(slot_count, key_rows, head_count, HEAD)
    value_heads = key_value[..., inner_width:].reshape(slot_count, key_rows, head_count, HEAD)
    scores = (
        jnp.einsum("sqhe,skhe->shqk", query_heads, key_heads, preferred_element_type=F32) * 0.125
    )
    row_max = jnp.max(scores, axis=-1, keepdims=True)
    exponent = jnp.exp(scores - row_max)
    totals = jnp.sum(exponent, axis=-1, keepdims=True)
    probs = (exponent / totals).astype(BF16)
    log_total = row_max + jnp.log(totals)
    mixed_rows = jnp.einsum("shqk,skhe->sqhe", probs, value_heads, preferred_element_type=F32)
    mixed_rows = mixed_rows.reshape(-1, inner_width).astype(BF16)
    residual_after = latent_rows + mm(mixed_rows, output_w).reshape(latent_rows.shape)
    normalized_rows = norm_rows(residual_after, gain_rows[2], shift_rows[2]).astype(BF16)
    shared_rows = gather_rows(lay, normalized_rows.reshape(-1, model))
    hidden_rows = mm(shared_rows, up_w)
    activated_rows = jax.nn.gelu(hidden_rows, approximate=False).astype(BF16)
    branch = return_rows(lay, mm(activated_rows, down_w))
    layer_result = residual_after + branch.reshape(latent_rows.shape)
    stored = (
        latent_rows,
        joined,
        query_heads,
        key_heads,
        value_heads,
        log_total,
        mixed_rows,
        residual_after,
        shared_rows,
        hidden_rows,
        activated_rows,
    )
    return (layer_result, stored)


def layer_backward(lay, upstream, media_float, current, stored):
    query_w, key_value_w, output_w, up_w, down_w, gain_rows, shift_rows = current
    (
        latent_rows,
        joined,
        query_heads,
        key_heads,
        value_heads,
        log_total,
        mixed_rows,
        residual_after,
        shared_rows,
        hidden_rows,
        activated_rows,
    ) = stored
    inner_width = query_w.shape[1]
    slot_count, query_rows, model = latent_rows.shape
    patch_rows = media_float.shape[1]
    key_rows = key_heads.shape[1]
    head_count = inner_width // HEAD
    branch_gradient = gather_rows(lay, upstream.astype(BF16).reshape(-1, model))
    down_term = mm_tn(activated_rows, branch_gradient).astype(BF16)
    activated_grad = mm_nt(branch_gradient, down_w)
    _, gelu_pull = jax.vjp(lambda inputs: jax.nn.gelu(inputs, approximate=False), hidden_rows)
    hidden_grad = gelu_pull(activated_grad)[0].astype(BF16)
    up_term = mm_tn(shared_rows, hidden_grad).astype(BF16)
    normed_grad = return_rows(lay, mm_nt(hidden_grad, up_w)).reshape(upstream.shape)
    feed_grads = reduce_feed(lay, up_term, down_term, model // lay.devices)
    _, feed_pull = jax.vjp(norm_rows, residual_after, gain_rows[2], shift_rows[2])
    d_after, gain_feed, shift_feed = feed_pull(normed_grad)
    d_after = d_after + upstream
    attention_grad = d_after.astype(BF16).reshape(-1, model)
    output_term = mm_tn(mixed_rows, attention_grad)
    mixed_grad = mm_nt(attention_grad, output_w)
    mixed_grad = mixed_grad.astype(BF16).reshape(slot_count, query_rows, head_count, HEAD)
    scores = (
        jnp.einsum("sqhe,skhe->shqk", query_heads, key_heads, preferred_element_type=F32) * 0.125
    )
    soft = jnp.exp(scores - log_total)
    probs = soft.astype(BF16)
    d_probs = jnp.einsum("sqhe,skhe->shqk", mixed_grad, value_heads, preferred_element_type=F32)
    d_values = jnp.einsum("shqk,sqhe->skhe", probs, mixed_grad, preferred_element_type=F32)
    d_scores = soft * (d_probs - jnp.sum(d_probs * soft, axis=-1, keepdims=True))
    d_scores = d_scores.astype(BF16)
    query_input_grad = (
        jnp.einsum("shqk,skhe->sqhe", d_scores, key_heads, preferred_element_type=F32) * 0.125
    )
    query_input_grad = query_input_grad.reshape(-1, inner_width).astype(BF16)
    d_keys = (
        jnp.einsum("shqk,sqhe->skhe", d_scores, query_heads, preferred_element_type=F32) * 0.125
    )
    d_pairs = jnp.concatenate(
        [
            d_keys.reshape(slot_count, key_rows, inner_width),
            d_values.reshape(slot_count, key_rows, inner_width),
        ],
        axis=-1,
    )
    parts = 2 ** len(lay.lat)
    d_pairs = jnp.moveaxis(d_pairs.reshape(slot_count, parts, key_rows // parts, -1), 1, 0)
    own_pairs, _ = shed(d_pairs, lay.lat, lay.lat)
    own_pairs = own_pairs.astype(BF16).reshape(-1, 2 * inner_width)
    flat_joined = joined.reshape(-1, model)
    key_value_term = mm_tn(flat_joined, own_pairs)
    d_joined = mm_nt(own_pairs, key_value_w).reshape(joined.shape)
    normed_latent_rows = joined[:, patch_rows:].reshape(-1, model)
    query_term = mm_tn(normed_latent_rows, query_input_grad)
    attention_grads = reduce_attention(lay, key_value_term, output_term, query_term)
    d_latent_norm = d_joined[:, patch_rows:] + mm_nt(query_input_grad, query_w).reshape(
        latent_rows.shape
    )
    _, media_pull = jax.vjp(norm_rows, media_float, gain_rows[0], shift_rows[0])
    d_media, gain_media, shift_media = media_pull(d_joined[:, :patch_rows])
    _, latent_pull = jax.vjp(norm_rows, latent_rows, gain_rows[1], shift_rows[1])
    d_latent, gain_latent, shift_latent = latent_pull(d_latent_norm)
    d_rows = d_latent + d_after
    norm_terms = ([gain_media, gain_latent, gain_feed], [shift_media, shift_latent, shift_feed])
    return (d_rows, d_media, attention_grads, feed_grads, norm_terms)


def make_device(lay):
    def per_device(
        media_tokens,
        image_counts,
        latent_init,
        cotangent,
        query_weight,
        key_value_weight,
        output_weight,
        up_weight,
        down_weight,
        norm_gain,
        norm_shift,
    ):
        slot_count = media_tokens.shape[0]
        model_width = media_tokens.shape[2]
        latent_count = latent_init.shape[0]
        position = jnp.arange(slot_count) % MEDIA
        per_slot = jnp.repeat(image_counts, MEDIA)
        valid_mask = (position < per_slot).astype(F32)[:, None, None]
        media_float = media_tokens.astype(F32)
        device = lax.axis_index("img") * lax.axis_size("lat") + lax.axis_index("lat")
        lanes = norm_gain.shape[-1]
        kinds = norm_gain.shape[1]
        norms = jnp.concatenate(
            [norm_gain.reshape(-1, lanes), norm_shift.reshape(-1, lanes)], axis=0
        )
        spread = jnp.zeros((16, model_width), BF16)
        spread = lax.dynamic_update_slice(spread, norms, (0, device * lanes))
        layers = []
        for level in range(LAYERS):
            extra = spread if level == 0 else None
            key_value_w, output_w, query_w, sums = gather_attention(
                lay, key_value_weight[level], output_weight[level], query_weight[level], extra
            )
            if level == 0:
                gain_all = sums[: LAYERS * kinds].reshape(LAYERS, kinds, model_width)
                shift_all = sums[LAYERS * kinds : 2 * LAYERS * kinds]
                shift_all = shift_all.reshape(LAYERS, kinds, model_width)
            up_w, down_w = gather_feed(lay, up_weight[level], down_weight[level])
            layers.append(
                (query_w, key_value_w, output_w, up_w, down_w, gain_all[level], shift_all[level])
            )
        latent_rows = jnp.broadcast_to(
            latent_init.astype(F32), (slot_count, latent_count, model_width)
        )
        stored_layers = []
        for level in range(LAYERS):
            latent_rows, stored = layer_forward(lay, latent_rows, media_float, layers[level])
            stored_layers.append(stored)
        resampled = latent_rows * valid_mask
        upstream = cotangent.astype(F32) * valid_mask
        media_grad = None
        attention = [None] * LAYERS
        feed = [None] * LAYERS
        terms = [None] * LAYERS
        for level in reversed(range(LAYERS)):
            upstream, d_media, attention[level], feed[level], terms[level] = layer_backward(
                lay, upstream, media_float, layers[level], stored_layers[level]
            )
            media_grad = d_media if media_grad is None else media_grad + d_media
        gains = [row for level in range(LAYERS) for row in terms[level][0]]
        shifts = [row for level in range(LAYERS) for row in terms[level][1]]
        small = jnp.stack(gains + shifts)
        pad = (-small.shape[0]) % 8
        small = jnp.pad(small, ((0, pad), (0, 0)))
        tail = jnp.concatenate([jnp.sum(upstream, axis=0), small], axis=0)
        tail = all_sum(tail, lay.img)
        latent_grad = tail[:latent_count]
        small = all_sum(tail[latent_count:], lay.lat)
        small = lax.dynamic_slice(small, (0, device * lanes), (2 * LAYERS * kinds, lanes))
        small = small.reshape(2, LAYERS, kinds, lanes)
        return (
            resampled,
            media_grad,
            latent_grad,
            jnp.stack([entry[2] for entry in attention]),
            jnp.stack([entry[0] for entry in attention]),
            jnp.stack([entry[1] for entry in attention]),
            jnp.stack([entry[0] for entry in feed]),
            jnp.stack([entry[1] for entry in feed]),
            small[0],
            small[1],
        )

    return per_device


def solution(mesh):
    lay = Layout(mesh.shape["img"], mesh.shape["lat"])
    in_specs = (
        P("img", "lat", None),
        P("img"),
        P("lat", None),
        P("img", "lat", None),
        P(None, ("img", "lat"), None),
        P(None, ("img", "lat"), None),
        P(None, ("img", "lat"), None),
        P(None, ("img", "lat"), None),
        P(None, ("img", "lat"), None),
        P(None, None, ("img", "lat")),
        P(None, None, ("img", "lat")),
    )
    out_specs = (
        P("img", "lat", None),
        P("img", "lat", None),
        P("lat", None),
        P(None, ("img", "lat"), None),
        P(None, ("img", "lat"), None),
        P(None, ("img", "lat"), None),
        P(None, ("img", "lat"), None),
        P(None, ("img", "lat"), None),
        P(None, None, ("img", "lat")),
        P(None, None, ("img", "lat")),
    )
    return jax.shard_map(
        make_device(lay), mesh=mesh, in_specs=in_specs, out_specs=out_specs, check_vma=False
    )
```

time: 3150 us -> 671 us (0.21)
  waiting for transfers between devices: 2610 us -> 259 us
  blocking collectives: 161 us -> 0 us
  matrix products: 162 us -> 82.3 us
  starting transfers between devices: 2.19 us -> 72 us
  other arithmetic: 59.8 us -> 95.7 us
    reduce_scatter x12 -> x0, waiting for transfers between devices: 1500 us -> none  [the longest x2 371 us: layer_backward(): lax.psum_scatter(down_contribution, ('img', 'lat'), scatter_dimension=0,...]
    unnamed x33 -> x0, waiting for transfers between devices: 531 us -> none
    all_gather x12 -> x0, waiting for transfers between devices: 472 us -> none  [the longest x2 152 us: per_device(): lax.all_gather(up_weight[level_index], ('img', 'lat'), axis=0, tiled=True)]
    ppermute x0 -> x89, waiting for transfers between devices: none -> 259 us  [swap(): return lax.ppermute(array, self.axis, self.pairs)]
    all_gather x4 -> x0, blocking collectives: 161 us -> none  [the longest x2 84.6 us: per_device(): lax.all_gather(norm_gain[level_index], ('img', 'lat'), axis=1, tiled=True)]
    psum x1 -> x0, waiting for transfers between devices: 111 us -> none  [per_device(): latent_grad = lax.psum(jnp.sum(upstream, axis=0), 'img')]
    dot_general x32, matrix products: 140 us -> 66 us  [the longest x10 22.1 us: mm(): lax.dot_general(a, b, (((1,), (0,)), ((), ())), preferred_element_type=F32)]
    ppermute x0 -> x89, starting transfers between devices: none -> 72 us  [swap(): return lax.ppermute(array, self.axis, self.pairs)]
  transfers between devices with their start and end apart: 29 -> 89, of which waited for: 27 -> 37; matrix products, arithmetic and copies ran while one was open for 8% -> 41% of each run, Pallas kernels for 0% -> 0%
where the time goes in v1:
time: 671 us; the launch traced here: 660 us
  waiting for transfers between devices  259 us (39%)
  local copies, waits for them, and re-layouts  145 us (22%)
  other arithmetic  95.7 us (14%)
  matrix products  82.3 us (12%)
  starting transfers between devices  72 us (11%)
    ppermute x89, waiting for transfers between devices, swap(): return lax.ppermute(array, self.axis, self.pairs)  259 us
    ppermute x89, starting transfers between devices, swap(): return lax.ppermute(array, self.axis, self.pairs)  72 us
    concatenate x8, local copies, waits for them, and re-layouts, layer_backward(): jnp.concatenate([d_keys.reshape(slot_count, key_rows, inner_width), d_val...  61.5 us
    another operation x71, other arithmetic, join(): jnp.stack([jnp.where(low, array, other), jnp.where(low, other, array)], a...  27.5 us
    unnamed x491, local copies, waits for them, and re-layouts  27.3 us
    dot_general x10, matrix products, mm(): lax.dot_general(a, b, (((1,), (0,)), ((), ())), preferred_element_type=F32)  22.1 us
    dot_general x10, matrix products, mm_nt(): lax.dot_general(a, b, (((1,), (1,)), ((), ())), preferred_element_type=F32)  20.2 us
    dot_general x10, matrix products, mm_tn(): lax.dot_general(a, b, (((0,), (0,)), ((), ())), preferred_element_type=F32)  18.2 us
  transfers between devices with their start and end apart: 89, of which 37 were waited for; matrix products, arithmetic and copies ran while one was open for 41% of the time, Pallas kernels for 0%

profile of v1, /device:TPU:0, one launch (start us, length us, event | category | flops | bytes accessed | tf_op | source)
XLA Modules:
  0.0 659.5 jit_solution(1981657957602331934)
XLA Ops:
  30.9 17.5 %collective-permute-done.12 = bf16[2,32,1024]{2,1,0:T(8,128)(2,1)S(1)} collective-permute-done((bf16[2,32,1024]{2,1,0:T(8,128)(2,1)S(1)}, bf16[2,32,1024]{2,1,0:T(8,128)(2,1)S(1)}, u32[]{:S(2)}, u32[]{:S(2)}) %collective-permute-start.12) | collective-permute-done | bytes 131104 | tf_op jit(solution)/shard_map/ppermute | solution.py:24
  48.4 6.3 collective-permute-done.33
  59.8 8.1 %collective-permute-done.1 = bf16[2,80,1024]{2,1,0:T(8,128)(2,1)S(1)} collective-permute-done((bf16[2,80,1024]{2,1,0:T(8,128)(2,1)S(1)}, bf16[2,80,1024]{2,1,0:T(8,128)(2,1)S(1)}, u32[]{:S(2)}, u32[]{:S(2)}) %collective-permute-start.1) | collective-permute-done | bytes 327712 | tf_op jit(solution)/shard_map/ppermute | solution.py:24
  71.4 5.8 collective-permute-done.5
  121.5 6.5 collective-permute-done.28
  148.3 5.5 collective-permute-done.9
  160.8 8.5 %multiply_convert_fusion.1 = (bf16[640,1024]{1,0:T(8,128)(2,1)S(1)}, f32[640,1024]{1,0:T(8,128)}, f32[640,1024]{1,0:T(8,128)}) fusion(bf16[640,1024]{1,0:T(8,128)(2,1)S(1)} %bitcast.840, bf16[1024,1024]{1,0:T(8,128)(2,1)S(1)} %bitcast.826), kind=kOutput, calls=%fused_computation.72 | convolution fusion | flops 1384775680 | bytes 9961472 | tf_op jit(solution)/shard_map/dot_general | solution.py:81
  178.8 8.7 %collective-permute-done.20 = bf16[160,1024]{1,0:T(8,128)(2,1)S(1)} collective-permute-done((bf16[160,1024]{1,0:T(8,128)(2,1)S(1)}, bf16[160,1024]{1,0:T(8,128)(2,1)S(1)}, u32[]{:S(2)}, u32[]{:S(2)}) %collective-permute-start.20) | collective-permute-done | bytes 327712 | tf_op jit(solution)/shard_map/ppermute | solution.py:24
  221.8 6.4 collective-permute-done.30
  241.8 7.9 %add_convert_fusion.1 = (bf16[640,1024]{1,0:T(8,128)(2,1)S(1)}, f32[640,1024]{1,0:T(8,128)S(1)}) fusion(f32[640,1024]{1,0:T(8,128)S(1)} %fusion.193, bf16[640,1024]{1,0:T(8,128)(2,1)S(1)} %bitcast.842, bf16[1024,1024]{1,0:T(8,128)(2,1)S(1)} %bitcast.830), kind=kOutput, calls=%fused_computation.58 | convolution fusion | flops 1389363200 | bytes 9961472 | tf_op jit(solution)/shard_map/dot_general | solution.py:85
  266.4 8.2 %collective-permute-done.45 = bf16[160,1024]{1,0:T(8,128)(2,1)S(1)} collective-permute-done((bf16[160,1024]{1,0:T(8,128)(2,1)S(1)}, bf16[160,1024]{1,0:T(8,128)(2,1)S(1)}, u32[]{:S(2)}, u32[]{:S(2)}) %collective-permute-start.45) | collective-permute-done | bytes 327712 | tf_op jit(solution)/shard_map/ppermute | solution.py:24
  301.6 7.6 %concatenate.156 = f32[5,2,160,512]{2,1,3,0:T(2,128)} reshape(f32[5,320,8,64]{1,3,2,0:T(8,128)} %convolution_bitcast_fusion.1) | data formatting | bytes 6553600 | tf_op jit(solution)/shard_map/concatenate | solution.py:330
  309.2 8.3 %copy.247 = f32[5,2,160,512]{3,2,1,0:T(8,128)} copy(f32[5,2,160,512]{2,1,3,0:T(2,128)} %concatenate.156) | data formatting | bytes 6553600 | tf_op jit(solution)/shard_map/concatenate | solution.py:330
  320.2 7.6 %concatenate.155 = f32[5,2,160,512]{2,1,3,0:T(2,128)} reshape(f32[5,320,8,64]{1,3,2,0:T(8,128)} %multiply_bitcast_fusion.1) | data formatting | bytes 6553600 | tf_op jit(solution)/shard_map/concatenate | solution.py:330
  327.8 8.2 %copy.246 = f32[5,2,160,512]{3,2,1,0:T(8,128)} copy(f32[5,2,160,512]{2,1,3,0:T(2,128)} %concatenate.155) | data formatting | bytes 6553600 | tf_op jit(solution)/shard_map/concatenate | solution.py:330
  342.4 10.3 %collective-permute-done.78 = bf16[2,2,2,32,1024]{4,3,2,1,0:T(8,128)(2,1)S(1)} collective-permute-done((bf16[2,2,2,32,1024]{4,3,2,1,0:T(8,128)(2,1)S(1)}, bf16[2,2,2,32,1024]{4,3,2,1,0:T(8,128)(2,1)S(1)}, u32[]{:S(2)}, u32[]{:S(2)}) %collective-permute-start.78) | collective-permute-done | bytes 524320 | tf_op jit(solution)/shard_map/ppermute | solution.py:24
  360.1 16.2 %collective-permute-done.79 = bf16[2,2,32,1024]{3,2,1,0:T(8,128)(2,1)S(1)} collective-permute-done((bf16[2,2,32,1024]{3,2,1,0:T(8,128)(2,1)S(1)}, bf16[2,2,32,1024]{3,2,1,0:T(8,128)(2,1)S(1)}, u32[]{:S(2)}, u32[]{:S(2)}) %collective-permute-start.79) | collective-permute-done | bytes 262176 | tf_op jit(solution)/shard_map/ppermute | solution.py:24
  393.0 6.9 %collective-permute-done.68 = bf16[2,2,2,32,1024]{4,3,0,1,2:T(8,128)(2,1)S(1)} collective-permute-done((bf16[2,2,2,32,1024]{4,3,0,1,2:T(8,128)(2,1)S(1)}, bf16[2,2,2,32,1024]{4,3,0,1,2:T(8,128)(2,1)S(1)}, u32[]{:S(2)}, u32[]{:S(2)}) %collective-permute-start.68) | collective-permute-done | bytes 524320 | tf_op jit(solution)/shard_map/ppermute | solution.py:24
  426.4 6.7 %collective-permute-done.65 = bf16[2,2,2,32,1024]{4,3,0,1,2:T(8,128)(2,1)S(1)} collective-permute-done((bf16[2,2,2,32,1024]{4,3,0,1,2:T(8,128)(2,1)S(1)}, bf16[2,2,2,32,1024]{4,3,0,1,2:T(8,128)(2,1)S(1)}, u32[]{:S(2)}, u32[]{:S(2)}) %collective-permute-start.65) | collective-permute-done | bytes 524320 | tf_op jit(solution)/shard_map/ppermute | solution.py:24
  434.3 20.8 %collective-permute-done.66 = bf16[2,2,32,1024]{3,2,0,1:T(8,128)(2,1)S(1)} collective-permute-done((bf16[2,2,32,1024]{3,2,0,1:T(8,128)(2,1)S(1)}, bf16[2,2,32,1024]{3,2,0,1:T(8,128)(2,1)S(1)}, u32[]{:S(2)}, u32[]{:S(2)}) %collective-permute-start.66) | collective-permute-done | bytes 262176 | tf_op jit(solution)/shard_map/ppermute | solution.py:24
  480.4 7.6 %concatenate.159 = f32[5,2,160,512]{2,1,3,0:T(2,128)} reshape(f32[5,320,8,64]{1,3,2,0:T(8,128)} %convolution_bitcast_fusion) | data formatting | bytes 6553600 | tf_op jit(solution)/shard_map/concatenate | solution.py:330
  488.0 6.5 copy.254
  494.4 7.6 %concatenate.158 = f32[5,2,160,512]{2,1,3,0:T(2,128)} reshape(f32[5,320,8,64]{1,3,2,0:T(8,128)} %multiply_bitcast_fusion) | data formatting | bytes 6553600 | tf_op jit(solution)/shard_map/concatenate | solution.py:330
  502.0 8.2 %copy.253 = f32[5,2,160,512]{3,2,1,0:T(8,128)} copy(f32[5,2,160,512]{2,1,3,0:T(2,128)} %concatenate.158) | data formatting | bytes 6553600 | tf_op jit(solution)/shard_map/concatenate | solution.py:330
  528.8 6.9 %collective-permute-done.73 = bf16[2,2,2,32,1024]{4,3,2,1,0:T(8,128)(2,1)S(1)} collective-permute-done((bf16[2,2,2,32,1024]{4,3,2,1,0:T(8,128)(2,1)S(1)}, bf16[2,2,2,32,1024]{4,3,2,1,0:T(8,128)(2,1)S(1)}, u32[]{:S(2)}, u32[]{:S(2)}) %collective-permute-start.73) | collective-permute-done | bytes 524320 | tf_op jit(solution)/shard_map/ppermute | solution.py:24
  539.2 15.3 %collective-permute-done.74 = bf16[2,2,32,1024]{3,2,1,0:T(8,128)(2,1)S(1)} collective-permute-done((bf16[2,2,32,1024]{3,2,1,0:T(8,128)(2,1)S(1)}, bf16[2,2,32,1024]{3,2,1,0:T(8,128)(2,1)S(1)}, u32[]{:S(2)}, u32[]{:S(2)}) %collective-permute-start.74) | collective-permute-done | bytes 262176 | tf_op jit(solution)/shard_map/ppermute | solution.py:24
  554.7 5.4 collective-permute-done.84
  567.0 12.1 %collective-permute-done.60 = bf16[2,2,2,32,1024]{4,3,2,1,0:T(8,128)(2,1)S(1)} collective-permute-done((bf16[2,2,2,32,1024]{4,3,2,1,0:T(8,128)(2,1)S(1)}, bf16[2,2,2,32,1024]{4,3,2,1,0:T(8,128)(2,1)S(1)}, u32[]{:S(2)}, u32[]{:S(2)}) %collective-permute-start.60) | collective-permute-done | bytes 524320 | tf_op jit(solution)/shard_map/ppermute | solution.py:24
  606.0 17.9 %collective-permute-done.53 = f32[48,1024]{1,0:T(8,128)S(1)} collective-permute-done((f32[48,1024]{1,0:T(8,128)S(1)}, f32[48,1024]{1,0:T(8,128)S(1)}, u32[]{:S(2)}, u32[]{:S(2)}) %collective-permute-start.53) | collective-permute-done | bytes 196640 | tf_op jit(solution)/shard_map/ppermute | solution.py:24
  629.9 9.3 %collective-permute-done.55 = f32[48,1024]{1,0:T(8,128)S(1)} collective-permute-done((f32[48,1024]{1,0:T(8,128)S(1)}, f32[48,1024]{1,0:T(8,128)S(1)}, u32[]{:S(2)}, u32[]{:S(2)}) %collective-permute-start.55) | collective-permute-done | bytes 196640 | tf_op jit(solution)/shard_map/ppermute | solution.py:24
  643.0 5.2 collective-permute-done.62
  649.6 7.5 %collective-permute-done.63 = bf16[64,1024]{1,0:T(8,128)(2,1)S(1)} collective-permute-done((bf16[64,1024]{1,0:T(8,128)(2,1)S(1)}, bf16[64,1024]{1,0:T(8,128)(2,1)S(1)}, u32[]{:S(2)}, u32[]{:S(2)}) %collective-permute-start.63) | collective-permute-done | bytes 131104 | tf_op jit(solution)/shard_map/ppermute | solution.py:24
  (1007 shorter events, 362.0 us)
Async XLA Ops:
  12.8 56.9 %collective-permute-start.42 = (bf16[160,1024]{1,0:T(8,128)(2,1)S(1)}, bf16[160,1024]{1,0:T(8,128)(2,1)S(1)}, u32[]{:S(2)}, u32[]{:S(2)}) collective-permute-start(bf16[160,1024]{1,0:T(8,128)(2,1)S(1)} %bitcast.851), channel_id=1, source_target_pairs={{0,8},{2,10},{4,12},{6,14},{8,0},{10,2},{12,4},{14,6},{16,24},{18,... | collective-permute-start | bytes 983048 | tf_op jit(solution)/shard_map/ppermute | solution.py:24
  21.6 33.9 %collective-permute-start.37 = (bf16[128,1024]{1,0:T(8,128)(2,1)}, bf16[128,1024]{1,0:T(8,128)(2,1)S(1)}, u32[]{:S(2)}, u32[]{:S(2)}) collective-permute-start(bf16[128,1024]{1,0:T(8,128)(2,1)} %get-tuple-element.170), channel_id=1, source_target_pairs={{0,16},{2,18},{4,20},{6,22},{8,24},{10,26},{12,28},{14,30},{16,0},... | collective-permute-start | bytes 786440 | tf_op jit(solution)/shard_map/ppermute | solution.py:24
  25.3 33.2 %collective-permute-start.16 = (bf16[128,1024]{1,0:T(8,128)(2,1)}, bf16[128,1024]{1,0:T(8,128)(2,1)S(1)}, u32[]{:S(2)}, u32[]{:S(2)}) collective-permute-start(bf16[128,1024]{1,0:T(8,128)(2,1)} %get-tuple-element.171), channel_id=1, source_target_pairs={{0,16},{2,18},{4,20},{6,22},{8,24},{10,26},{12,28},{14,30},{16,0},... | collective-permute-start | bytes 786440 | tf_op jit(solution)/shard_map/ppermute | solution.py:24
  26.7 56.5 %collective-permute-start.22 = (bf16[2,64,1024]{2,1,0:T(8,128)(2,1)S(1)}, bf16[2,64,1024]{2,1,0:T(8,128)(2,1)S(1)}, u32[]{:S(2)}, u32[]{:S(2)}) collective-permute-start(bf16[2,64,1024]{2,1,0:T(8,128)(2,1)S(1)} %pad_maximum_fusion.44), channel_id=1, source_target_pairs={{0,8},{2,10},{4,12},{6,14},{8,0},{10,2},{12,4},{14,6},{16,24},{18,... | collective-permute-start | bytes 786440 | tf_op jit(solution)/shard_map/ppermute | solution.py:24
  55.5 116.5 %collective-permute-start.34 = (bf16[2,2,32,1024]{3,2,0,1:T(8,128)(2,1)}, bf16[2,2,32,1024]{3,2,0,1:T(8,128)(2,1)}, u32[]{:S(2)}, u32[]{:S(2)}) collective-permute-start(bf16[2,2,32,1024]{3,2,0,1:T(8,128)(2,1)} %pad_maximum_fusion.46), channel_id=1, source_target_pairs={{0,16},{2,18},{4,20},{6,22},{8,24},{10,26},{12,28},{14,30},{16,0},... | collective-permute-start | bytes 786440 | tf_op jit(solution)/shard_map/ppermute | solution.py:24
  58.5 35.7 %collective-permute-start.13 = (bf16[2,2,32,1024]{3,2,0,1:T(8,128)(2,1)S(1)}, bf16[2,2,32,1024]{3,2,0,1:T(8,128)(2,1)S(1)}, u32[]{:S(2)}, u32[]{:S(2)}) collective-permute-start(bf16[2,2,32,1024]{3,2,0,1:T(8,128)(2,1)S(1)} %pad_maximum_fusion.43), channel_id=1, source_target_pairs={{0,16},{2,18},{4,20},{6,22},{8,24},{10,26},{12,28},{14,30},{16,0},... | collective-permute-start | bytes 786440 | tf_op jit(solution)/shard_map/ppermute | solution.py:24
  83.2 31.0 %collective-permute-start.17 = (bf16[2,128,1024]{2,1,0:T(8,128)(2,1)S(1)}, bf16[2,128,1024]{2,1,0:T(8,128)(2,1)S(1)}, u32[]{:S(2)}, u32[]{:S(2)}) collective-permute-start(bf16[2,128,1024]{2,1,0:T(8,128)(2,1)S(1)} %pad_maximum_fusion.34), channel_id=1, source_target_pairs={{0,4},{2,6},{4,0},{6,2},{8,12},{10,14},{12,8},{14,10},{16,20},{18,... | collective-permute-start | bytes 1572872 | tf_op jit(solution)/shard_map/ppermute | solution.py:24
  103.2 70.0 %collective-permute-start.38 = (bf16[2,128,1024]{2,1,0:T(8,128)(2,1)}, bf16[2,128,1024]{2,1,0:T(8,128)(2,1)}, u32[]{:S(2)}, u32[]{:S(2)}) collective-permute-start(bf16[2,128,1024]{2,1,0:T(8,128)(2,1)} %pad_maximum_fusion.38), channel_id=1, source_target_pairs={{0,4},{2,6},{4,0},{6,2},{8,12},{10,14},{12,8},{14,10},{16,20},{18,... | collective-permute-start | bytes 1572872 | tf_op jit(solution)/shard_map/ppermute | solution.py:24
  105.8 22.2 %collective-permute-start.28 = (bf16[2,2,2,32,1024]{4,3,1,0,2:T(8,128)(2,1)S(1)}, bf16[2,2,2,32,1024]{4,3,1,0,2:T(8,128)(2,1)S(1)}, u32[]{:S(2)}, u32[]{:S(2)}) collective-permute-start(bf16[2,2,2,32,1024]{4,3,1,0,2:T(8,128)(2,1)S(1)} %pad_maximum_fusion.36), channel_id=1, source_target_pairs={{0,2},{2,0},{4,6},{6,4},{8,10},{10,8},{12,14},{14,12},{16,18},{18,... | collective-permute-start | bytes 1572872 | tf_op jit(solution)/shard_map/ppermute | solution.py:24
  119.7 26.9 %collective-permute-start.24 = (bf16[2,2,2,32,1024]{4,3,1,0,2:T(8,128)(2,1)}, bf16[2,2,2,32,1024]{4,3,1,0,2:T(8,128)(2,1)}, u32[]{:S(2)}, u32[]{:S(2)}) collective-permute-start(bf16[2,2,2,32,1024]{4,3,1,0,2:T(8,128)(2,1)} %pad_maximum_fusion.35), channel_id=1, source_target_pairs={{0,4},{2,6},{4,0},{6,2},{8,12},{10,14},{12,8},{14,10},{16,20},{18,... | collective-permute-start | bytes 1572872 | tf_op jit(solution)/shard_map/ppermute | solution.py:24
  128.0 25.9 %collective-permute-start.18 = (bf16[2,2,128,1024]{3,2,0,1:T(8,128)(2,1)}, bf16[2,2,128,1024]{3,2,0,1:T(8,128)(2,1)}, u32[]{:S(2)}, u32[]{:S(2)}) collective-permute-start(bf16[2,2,128,1024]{3,2,0,1:T(8,128)(2,1)} %pad_maximum_fusion.20), channel_id=1, source_target_pairs={{0,2},{2,0},{4,6},{6,4},{8,10},{10,8},{12,14},{14,12},{16,18},{18,... | collective-permute-start | bytes 3145736 | tf_op jit(solution)/shard_map/ppermute | solution.py:24
  131.4 25.0 %collective-permute-start.15 = (bf16[2,2,2,2,32,1024]{5,4,1,0,3,2:T(8,128)(2,1)}, bf16[2,2,2,2,32,1024]{5,4,1,0,3,2:T(8,128)(2,1)}, u32[]{:S(2)}, u32[]{:S(2)}) collective-permute-start(bf16[2,2,2,2,32,1024]{5,4,1,0,3,2:T(8,128)(2,1)} %pad_maximum_fusion.19), channel_id=1, source_target_pairs={{0,4},{2,6},{4,0},{6,2},{8,12},{10,14},{12,8},{14,10},{16,20},{18,... | collective-permute-start | bytes 3145736 | tf_op jit(solution)/shard_map/ppermute | solution.py:24
  153.8 38.4 %collective-permute-start.43 = (bf16[2,160,1024]{2,1,0:T(8,128)(2,1)S(1)}, bf16[2,160,1024]{2,1,0:T(8,128)(2,1)S(1)}, u32[]{:S(2)}, u32[]{:S(2)}) collective-permute-start(bf16[2,160,1024]{2,1,0:T(8,128)(2,1)S(1)} %copy-done.123), channel_id=1, source_target_pairs={{0,1},{1,0},{2,3},{3,2},{4,5},{5,4},{6,7},{7,6},{8,9},{9,8},{10,11... | collective-permute-start | bytes 1966088 | tf_op jit(solution)/shard_map/ppermute | solution.py:24
  177.3 41.4 %collective-permute-start.39 = (bf16[2,2,128,1024]{3,2,0,1:T(8,128)(2,1)}, bf16[2,2,128,1024]{3,2,0,1:T(8,128)(2,1)}, u32[]{:S(2)}, u32[]{:S(2)}) collective-permute-start(bf16[2,2,128,1024]{3,2,0,1:T(8,128)(2,1)} %pad_maximum_fusion.25), channel_id=1, source_target_pairs={{0,2},{2,0},{4,6},{6,4},{8,10},{10,8},{12,14},{14,12},{16,18},{18,... | collective-permute-start | bytes 3145736 | tf_op jit(solution)/shard_map/ppermute | solution.py:24
  195.1 34.3 %collective-permute-start.36 = (bf16[2,2,2,2,32,1024]{5,4,1,0,3,2:T(8,128)(2,1)}, bf16[2,2,2,2,32,1024]{5,4,1,0,3,2:T(8,128)(2,1)}, u32[]{:S(2)}, u32[]{:S(2)}) collective-permute-start(bf16[2,2,2,2,32,1024]{5,4,1,0,3,2:T(8,128)(2,1)} %pad_maximum_fusion.24), channel_id=1, source_target_pairs={{0,4},{2,6},{4,0},{6,2},{8,12},{10,14},{12,8},{14,10},{16,20},{18,... | collective-permute-start | bytes 3145736 | tf_op jit(solution)/shard_map/ppermute | solution.py:24
  260.4 78.2 %collective-permute-start.85 = (bf16[2,2,128,1024]{3,2,0,1:T(8,128)(2,1)}, bf16[2,2,128,1024]{3,2,0,1:T(8,128)(2,1)}, u32[]{:S(2)}, u32[]{:S(2)}) collective-permute-start(bf16[2,2,128,1024]{3,2,0,1:T(8,128)(2,1)} %bitcast.770), channel_id=1, source_target_pairs={{0,2},{2,0},{4,6},{6,4},{8,10},{10,8},{12,14},{14,12},{16,18},{18,... | collective-permute-start | bytes 3145736 | tf_op jit(solution)/shard_map/ppermute | solution.py:24
  263.2 72.8 %collective-permute-start.77 = (bf16[2,2,2,2,32,1024]{5,4,3,2,1,0:T(8,128)(2,1)}, bf16[2,2,2,2,32,1024]{5,4,3,2,1,0:T(8,128)(2,1)}, u32[]{:S(2)}, u32[]{:S(2)}) collective-permute-start(bf16[2,2,2,2,32,1024]{5,4,3,2,1,0:T(8,128)(2,1)} %dynamic-slice_bitcast_fusion), channel_id=1, source_target_pairs={{0,4},{2,6},{4,0},{6,2},{8,12},{10,14},{12,8},{14,10},{16,20},{18,... | collective-permute-start | bytes 3145736 | tf_op jit(solution)/shard_map/ppermute | solution.py:24
  298.8 85.0 %collective-permute-start.67 = (bf16[2,2,2,2,32,1024]{5,4,0,1,2,3:T(8,128)(2,1)}, bf16[2,2,2,2,32,1024]{5,4,0,1,2,3:T(8,128)(2,1)}, u32[]{:S(2)}, u32[]{:S(2)}) collective-permute-start(bf16[2,2,2,2,32,1024]{5,4,0,1,2,3:T(8,128)(2,1)} %bitcast.769), channel_id=1, source_target_pairs={{0,1},{1,0},{2,3},{3,2},{4,5},{5,4},{6,7},{7,6},{8,9},{9,8},{10,11... | collective-permute-start | bytes 3145736 | tf_op jit(solution)/shard_map/ppermute | solution.py:24
  342.3 44.5 %collective-permute-start.46 = (bf16[5,160,1024]{2,1,0:T(8,128)(2,1)S(1)}, bf16[5,160,1024]{2,1,0:T(8,128)(2,1)S(1)}, u32[]{:S(2)}, u32[]{:S(2)}) collective-permute-start(bf16[5,160,1024]{2,1,0:T(8,128)(2,1)S(1)} %fusion.47), channel_id=1, source_target_pairs={{0,1},{1,0},{2,3},{3,2},{4,5},{5,4},{6,7},{7,6},{8,9},{9,8},{10,11... | collective-permute-start | bytes 4915208 | tf_op jit(solution)/shard_map/ppermute | solution.py:24
  352.9 23.4 %collective-permute-start.79 = (bf16[2,2,32,1024]{3,2,1,0:T(8,128)(2,1)S(1)}, bf16[2,2,32,1024]{3,2,1,0:T(8,128)(2,1)S(1)}, u32[]{:S(2)}, u32[]{:S(2)}) collective-permute-start(bf16[2,2,32,1024]{3,2,1,0:T(8,128)(2,1)S(1)} %fusion.128), channel_id=1, source_target_pairs={{0,16},{2,18},{4,20},{6,22},{8,24},{10,26},{12,28},{14,30},{16,0},... | collective-permute-start | bytes 786440 | tf_op jit(solution)/shard_map/ppermute | solution.py:24
  358.1 22.8 %collective-permute-start.87 = (bf16[128,1024]{1,0:T(8,128)(2,1)S(1)}, bf16[128,1024]{1,0:T(8,128)(2,1)S(1)}, u32[]{:S(2)}, u32[]{:S(2)}) collective-permute-start(bf16[128,1024]{1,0:T(8,128)(2,1)S(1)} %fusion.130), channel_id=1, source_target_pairs={{0,16},{2,18},{4,20},{6,22},{8,24},{10,26},{12,28},{14,30},{16,0},... | collective-permute-start | bytes 786440 | tf_op jit(solution)/shard_map/ppermute | solution.py:24
  424.1 88.5 %collective-permute-start.82 = (bf16[2,2,128,1024]{3,2,0,1:T(8,128)(2,1)}, bf16[2,2,128,1024]{3,2,0,1:T(8,128)(2,1)}, u32[]{:S(2)}, u32[]{:S(2)}) collective-permute-start(bf16[2,2,128,1024]{3,2,0,1:T(8,128)(2,1)} %bitcast.771), channel_id=1, source_target_pairs={{0,2},{2,0},{4,6},{6,4},{8,10},{10,8},{12,14},{14,12},{16,18},{18,... | collective-permute-start | bytes 3145736 | tf_op jit(solution)/shard_map/ppermute | solution.py:24
  425.7 94.9 %collective-permute-start.72 = (bf16[2,2,2,2,32,1024]{5,4,3,2,1,0:T(8,128)(2,1)}, bf16[2,2,2,2,32,1024]{5,4,3,2,1,0:T(8,128)(2,1)}, u32[]{:S(2)}, u32[]{:S(2)}) collective-permute-start(bf16[2,2,2,2,32,1024]{5,4,3,2,1,0:T(8,128)(2,1)} %dynamic-slice_bitcast_fusion.1), channel_id=1, source_target_pairs={{0,4},{2,6},{4,0},{6,2},{8,12},{10,14},{12,8},{14,10},{16,20},{18,... | collective-permute-start | bytes 3145736 | tf_op jit(solution)/shard_map/ppermute | solution.py:24
  433.3 21.9 %collective-permute-start.66 = (bf16[2,2,32,1024]{3,2,0,1:T(8,128)(2,1)S(1)}, bf16[2,2,32,1024]{3,2,0,1:T(8,128)(2,1)S(1)}, u32[]{:S(2)}, u32[]{:S(2)}) collective-permute-start(bf16[2,2,32,1024]{3,2,0,1:T(8,128)(2,1)S(1)} %fusion.125), channel_id=1, source_target_pairs={{0,2},{2,0},{4,6},{6,4},{8,10},{10,8},{12,14},{14,12},{16,18},{18,... | collective-permute-start | bytes 786440 | tf_op jit(solution)/shard_map/ppermute | solution.py:24
  434.3 21.9 %collective-permute-start.50 = (bf16[160,1024]{1,0:T(8,128)(2,1)S(1)}, bf16[160,1024]{1,0:T(8,128)(2,1)S(1)}, u32[]{:S(2)}, u32[]{:S(2)}) collective-permute-start(bf16[160,1024]{1,0:T(8,128)(2,1)S(1)} %fusion.110), channel_id=1, source_target_pairs={{0,8},{2,10},{4,12},{6,14},{8,0},{10,2},{12,4},{14,6},{16,24},{18,... | collective-permute-start | bytes 983048 | tf_op jit(solution)/shard_map/ppermute | solution.py:24
  456.1 59.3 %collective-permute-start.70 = (bf16[2,64,1024]{2,1,0:T(8,128)(2,1)}, bf16[2,64,1024]{2,1,0:T(8,128)(2,1)}, u32[]{:S(2)}, u32[]{:S(2)}) collective-permute-start(bf16[2,64,1024]{2,1,0:T(8,128)(2,1)} %fusion.133), channel_id=1, source_target_pairs={{0,8},{2,10},{4,12},{6,14},{8,0},{10,2},{12,4},{14,6},{16,24},{18,... | collective-permute-start | bytes 786440 | tf_op jit(solution)/shard_map/ppermute | solution.py:24
  480.4 82.7 %collective-permute-start.59 = (bf16[2,2,2,2,32,1024]{5,4,3,2,1,0:T(8,128)(2,1)}, bf16[2,2,2,2,32,1024]{5,4,3,2,1,0:T(8,128)(2,1)}, u32[]{:S(2)}, u32[]{:S(2)}) collective-permute-start(bf16[2,2,2,2,32,1024]{5,4,3,2,1,0:T(8,128)(2,1)} %dynamic-slice_bitcast_fusion.2), channel_id=1, source_target_pairs={{0,1},{1,0},{2,3},{3,2},{4,5},{5,4},{6,7},{7,6},{8,9},{9,8},{10,11... | collective-permute-start | bytes 3145736 | tf_op jit(solution)/shard_map/ppermute | solution.py:24
  512.0 68.3 %collective-permute-start.51 = (bf16[5,160,1024]{2,1,0:T(8,128)(2,1)S(1)}, bf16[5,160,1024]{2,1,0:T(8,128)(2,1)S(1)}, u32[]{:S(2)}, u32[]{:S(2)}) collective-permute-start(bf16[5,160,1024]{2,1,0:T(8,128)(2,1)S(1)} %fusion.48), channel_id=1, source_target_pairs={{0,1},{1,0},{2,3},{3,2},{4,5},{5,4},{6,7},{7,6},{8,9},{9,8},{10,11... | collective-permute-start | bytes 4915208 | tf_op jit(solution)/shard_map/ppermute | solution.py:24
  514.4 22.0 %collective-permute-start.83 = (bf16[2,128,1024]{2,1,0:T(8,128)(2,1)S(1)}, bf16[2,128,1024]{2,1,0:T(8,128)(2,1)S(1)}, u32[]{:S(2)}, u32[]{:S(2)}) collective-permute-start(bf16[2,128,1024]{2,1,0:T(8,128)(2,1)S(1)} %fusion.87), channel_id=1, source_target_pairs={{0,4},{2,6},{4,0},{6,2},{8,12},{10,14},{12,8},{14,10},{16,20},{18,... | collective-permute-start | bytes 1572872 | tf_op jit(solution)/shard_map/ppermute | solution.py:24
  536.6 23.6 %collective-permute-start.84 = (bf16[128,1024]{1,0:T(8,128)(2,1)S(1)}, bf16[128,1024]{1,0:T(8,128)(2,1)S(1)}, u32[]{:S(2)}, u32[]{:S(2)}) collective-permute-start(bf16[128,1024]{1,0:T(8,128)(2,1)S(1)} %fusion.129), channel_id=1, source_target_pairs={{0,16},{2,18},{4,20},{6,22},{8,24},{10,26},{12,28},{14,30},{16,0},... | collective-permute-start | bytes 786440 | tf_op jit(solution)/shard_map/ppermute | solution.py:24
  600.8 23.3 %collective-permute-start.57 = (bf16[2,2,2,32,1024]{4,3,1,0,2:T(8,128)(2,1)S(1)}, bf16[2,2,2,32,1024]{4,3,1,0,2:T(8,128)(2,1)S(1)}, u32[]{:S(2)}, u32[]{:S(2)}) collective-permute-start(bf16[2,2,2,32,1024]{4,3,1,0,2:T(8,128)(2,1)S(1)} %fusion.81), channel_id=1, source_target_pairs={{0,4},{2,6},{4,0},{6,2},{8,12},{10,14},{12,8},{14,10},{16,20},{18,... | collective-permute-start | bytes 1572872 | tf_op jit(solution)/shard_map/ppermute | solution.py:24
  601.9 28.0 %collective-permute-start.61 = (bf16[2,2,32,1024]{3,2,1,0:T(8,128)(2,1)S(1)}, bf16[2,2,32,1024]{3,2,1,0:T(8,128)(2,1)S(1)}, u32[]{:S(2)}, u32[]{:S(2)}) collective-permute-start(bf16[2,2,32,1024]{3,2,1,0:T(8,128)(2,1)S(1)} %fusion.124), channel_id=1, source_target_pairs={{0,4},{2,6},{4,0},{6,2},{8,12},{10,14},{12,8},{14,10},{16,20},{18,... | collective-permute-start | bytes 786440 | tf_op jit(solution)/shard_map/ppermute | solution.py:24
  (262 other events, 2080.5 us)

commit v2 on v1

v2 whole, which is shorter than its diff:
```python
import jax
import jax.numpy as jnp
from jax import lax
from jax.experimental import pallas as pl
from jax.experimental.pallas import tpu as pltpu
from jax.sharding import PartitionSpec as P

HEAD = 64
MEDIA = 5
LAYERS = 2
F32 = jnp.float32
BF16 = jnp.bfloat16
NORM_ROWS = 16


class Order:
    def __init__(self, token):
        self.token = token

    def gate(self, *arrays):
        arrays = lax.optimization_barrier(arrays + (self.token,))
        self.token = arrays[-1]
        return arrays[:-1] if len(arrays) > 2 else arrays[0]

    def all(self, arrays):
        arrays = lax.optimization_barrier(tuple(arrays) + (self.token,))
        self.token = arrays[-1]
        return list(arrays[:-1])

    def send(self, swap, array):
        return swap(self.gate(array))


class Bit:
    def __init__(self, axis, size, place, rank):
        self.rank = rank
        self.axis = axis
        self.mask = 1 << place
        self.pairs = [(source, source ^ self.mask) for source in range(size)]

    def mine(self):
        return (lax.axis_index(self.axis) // self.mask) % 2

    def swap(self, array):
        return lax.ppermute(array, self.axis, self.pairs)


class Four:
    def __init__(self, size, place):
        self.shift = 1 << place
        self.swaps = [self._swap(size, mask) for mask in (1, 2, 3)]

    def _swap(self, size, mask):
        pairs = [(source, source ^ (mask * self.shift)) for source in range(size)]
        return lambda array: lax.ppermute(array, "img", pairs)

    def mine(self):
        return (lax.axis_index("img") // self.shift) % 4

    def spread(self, order, array):
        return [order.send(swap, array) for swap in self.swaps]

    def merge(self, own, others, axis):
        pieces = [own] + others
        low = self.mine() % 2 == 0
        high = self.mine() // 2 == 0
        mixed = [
            [jnp.where(low, pieces[2 * a + b], pieces[2 * a + 1 - b]) for b in range(2)]
            for a in range(2)
        ]
        return jnp.stack(
            [jnp.where(high, mixed[c][b], mixed[1 - c][b]) for c in range(2) for b in range(2)],
            axis=axis,
        )

    def shed(self, order, terms, axis):
        me = self.mine()
        terms = list(order.all(terms))
        others = []
        for mask, swap in zip((1, 2, 3), self.swaps):
            sent = total([pick(term, me ^ mask, axis) for term in terms]).astype(BF16)
            others.append(order.send(swap, sent))
        return [pick(term, me, axis) for term in terms] + others


class Layout:
    def __init__(self, img, lat):
        lat_bits = [Bit("lat", lat, k, k) for k in range(lat.bit_length() - 1)]
        img_bits = [Bit("img", img, k, k + len(lat_bits)) for k in range(img.bit_length() - 1)]
        self.devices = img * lat
        self.lat = lat_bits[0]
        self.img = img_bits
        self.every = list(reversed(lat_bits + img_bits))
        self.first, self.second = img_bits[0], img_bits[1]
        self.far = list(reversed(img_bits[3:]))
        self.beyond = list(reversed(img_bits[4:]))
        self.plane = Four(img, 0)
        self.column = Four(img, 2)
        self.tensor = [img_bits[2], lat_bits[0]]
        self.split = 4
        self.outer = img // 16


def pick(array, index, axis):
    return lax.dynamic_index_in_dim(array, index, axis, keepdims=False)


def part(array, bit, place, own):
    return pick(array, bit.mine() if own else 1 - bit.mine(), place)


def pair(bit, own, other, axis):
    low = bit.mine() == 0
    return jnp.stack([jnp.where(low, own, other), jnp.where(low, other, own)], axis=axis)


def join(order, array, bits, have):
    have = list(have)
    for bit in bits:
        other = order.send(bit.swap, array)
        place = sum(1 for held in have if held.rank > bit.rank)
        array = pair(bit, array, other, place)
        have.insert(place, bit)
    return array, have


def total(terms):
    value = terms[0].astype(F32)
    for term in terms[1:]:
        value = value + term.astype(F32)
    return value


def shed(order, terms, bit, have):
    place = have.index(bit)
    terms = order.all(terms)
    sent = total([part(term, bit, place, False) for term in terms]).astype(BF16)
    other = order.send(bit.swap, sent)
    terms = [part(term, bit, place, True) for term in terms] + [other]
    return terms, [held for held in have if held is not bit]


def exchange(order, array, bit, place):
    other = order.send(bit.swap, part(array, bit, place, False))
    return pair(bit, part(array, bit, place, True), other, place)


def mm(a, b):
    return lax.dot_general(a, b, (((1,), (0,)), ((), ())), preferred_element_type=F32)


def mm_nt(a, b):
    return lax.dot_general(a, b, (((1,), (1,)), ((), ())), preferred_element_type=F32)


def mm_tn(a, b):
    return lax.dot_general(a, b, (((0,), (0,)), ((), ())), preferred_element_type=F32)


class Attention:
    def __init__(self, lay, order, kv_shard, out_shard, query_shard, extra):
        self.lay, self.order = lay, order
        self.rows, self.width = kv_shard.shape
        self.out_rows = out_shard.shape[0]
        half = self.width // 2
        outs = jnp.concatenate([out_shard[:, :half], out_shard[:, half:]], axis=0)
        parts = [kv_shard, jnp.concatenate([query_shard, outs], axis=1)]
        if extra is not None:
            parts.append(extra)
        self.extra = extra is not None
        self.own = jnp.concatenate(parts, axis=0)

    def start_column(self):
        lay = self.lay
        self.own, _ = join(self.order, self.own, lay.beyond, [])
        self.own = self.own.reshape((lay.outer,) + self.own.shape[-2:])
        self.others = lay.column.spread(self.order, self.own)

    def end_column(self):
        own, *others = self.order.all([self.own] + self.others)
        self.own = self.lay.column.merge(own, others, 1)

    def start_plane(self):
        self.others = self.lay.plane.spread(self.order, self.own)

    def end_plane(self):
        own, *others = self.order.all([self.own] + self.others)
        self.own = self.lay.plane.merge(own, others, 2)

    def start_lat(self):
        self.others = self.order.send(self.lay.lat.swap, self.own)

    def end_lat(self):
        lay, rows, width = self.lay, self.rows, self.width
        half = width // 2
        self.own, self.others = self.order.gate(self.own, self.others)

        def both(select):
            return pair(lay.lat, select(self.own), select(self.others), 3)

        key_value = both(lambda a: a[..., :rows, :]).reshape(-1, width)
        query = both(lambda a: a[..., rows : 2 * rows, :half]).reshape(-1, half)
        middle = rows + self.out_rows
        output = both(
            lambda a: jnp.concatenate(
                [a[..., rows:middle, half:], a[..., middle : 2 * rows, half:]], axis=-1
            )
        ).reshape(-1, width)
        if self.extra:
            own = self.own[..., 2 * rows :, :].astype(F32)
            other = self.others[..., 2 * rows :, :].astype(F32)
            self.norms = jnp.sum(own, axis=(0, 1, 2)) + jnp.sum(other, axis=(0, 1, 2))
        return query, key_value, output


def feed_columns(lay, array, forward):
    width = array.shape[-1] // lay.devices if forward else None
    ranks = [bit.rank for bit in lay.tensor]
    owner = []
    for device in range(lay.devices):
        value = 0
        for rank in ranks:
            value = value * 2 + (device >> rank) % 2
        owner.append(value)
    if forward:
        blocks = [array[..., d * width : (d + 1) * width] for d in range(lay.devices)]
        sets = [
            jnp.concatenate([blocks[d] for d in range(lay.devices) if owner[d] == s], axis=-1)
            for s in range(lay.split)
        ]
        return jnp.stack(sets)
    width = array.shape[-1] * lay.split // lay.devices
    seen = [0] * lay.split
    blocks = []
    for device in range(lay.devices):
        s = owner[device]
        blocks.append(array[s, :, seen[s] * width : (seen[s] + 1) * width])
        seen[s] += 1
    return jnp.concatenate(blocks, axis=-1)


class Feed:
    def __init__(self, lay, order, up_shard, down_shard):
        self.lay, self.order = lay, order
        self.rows = up_shard.shape[0]
        self.columns = up_shard.shape[1] // lay.split
        up = feed_columns(lay, up_shard, True)
        self.up = up.reshape((2, 2, self.rows, self.columns))
        self.down = down_shard

    def start_lat(self):
        self.other = self.order.send(self.lay.lat.swap, part(self.up, self.lay.lat, 1, False))

    def start_near(self):
        self.up, self.other = self.order.gate(self.up, self.other)
        own = part(self.up, self.lay.lat, 1, True)
        self.up = pair(self.lay.lat, own, self.other, 1)
        near = self.lay.tensor[0]
        self.other = self.order.send(near.swap, part(self.up, near, 0, False))

    def start_far(self):
        near = self.lay.tensor[0]
        self.up, self.other = self.order.gate(self.up, self.other)
        up = pair(near, part(self.up, near, 0, True), self.other, 0)
        packed = jnp.concatenate([up.reshape(-1, self.columns), self.down], axis=0)
        packed, self.have = join(self.order, packed, self.lay.far[:-1], [])
        self.own = packed
        self.other = self.order.send(self.lay.far[-1].swap, packed)

    def end_far(self):
        place = len(self.have)
        self.own, self.other = self.order.gate(self.own, self.other)
        packed = pair(self.lay.far[-1], self.own, self.other, place)
        self.have = self.have + [self.lay.far[-1]]
        cut = self.rows * self.lay.split
        up = packed[..., :cut, :]
        self.up = up.reshape((2,) * (len(self.have) + 2) + (self.rows, self.columns))
        self.down = packed[..., cut:, :]

    def start_plane(self):
        lay = self.lay
        self.up_other = self.order.send(lay.first.swap, self.up)
        self.down_other = self.order.send(lay.second.swap, self.down)

    def gate(self):
        arrays = [self.up, self.up_other, self.down, self.down_other]
        self.up, self.up_other, self.down, self.down_other = self.order.all(arrays)

    def next_plane(self):
        lay = self.lay
        place = len(self.have)
        self.gate()
        self.up = pair(lay.first, self.up, self.up_other, place + 1)
        self.down = pair(lay.second, self.down, self.down_other, place)
        self.up_other = self.order.send(lay.second.swap, self.up)
        self.down_other = self.order.send(lay.first.swap, self.down)

    def end_plane(self):
        lay = self.lay
        place = len(self.have)
        self.gate()
        up = pair(lay.second, self.up, self.up_other, place + 1)
        down = pair(lay.first, self.down, self.down_other, place + 1)
        return up.reshape(-1, self.columns), down.reshape(-1, self.columns)


class FeedGrad:
    def __init__(self, lay, order, up_term, down_term, rows):
        self.lay, self.order, self.rows = lay, order, rows
        self.columns = up_term.shape[1]
        self.up_have = lay.every
        self.up = [up_term.reshape((2,) * len(lay.every) + (rows, self.columns))]
        self.down_have = [bit for bit in lay.every if bit not in lay.tensor]
        self.down = [down_term.reshape((2,) * len(self.down_have) + (-1, self.columns))]

    def plane(self, turn):
        lay = self.lay
        bits = (lay.second, lay.first) if turn == 0 else (lay.first, lay.second)
        self.up, self.up_have = shed(self.order, self.up, bits[0], self.up_have)
        self.down, self.down_have = shed(self.order, self.down, bits[1], self.down_have)

    def far(self):
        lay = self.lay
        lead = (2,) * len(lay.far)
        count = len(self.up)
        both = self.order.all(self.up + self.down)
        self.up, self.down = both[:count], both[count:]
        terms = []
        for up, down in zip(self.up, self.down):
            up = up.reshape(lead + (-1, self.columns))
            terms.append(jnp.concatenate([up, down], axis=-2))
        have = list(lay.far)
        for bit in reversed(lay.far):
            terms, have = shed(self.order, terms, bit, have)
        self.terms = terms

    def start_near(self):
        cut = self.rows * self.lay.split
        packed = total(self.order.all(self.terms))
        self.down = packed[cut:]
        self.up = packed[:cut].astype(BF16).reshape(2, 2, self.rows, self.columns)
        near = self.lay.tensor[0]
        self.other = self.order.send(near.swap, part(self.up, near, 0, False))

    def start_lat(self):
        near, lat = self.lay.tensor
        self.up, self.other = self.order.gate(self.up, self.other)
        self.up = pair(near, part(self.up, near, 0, True), self.other, 0)
        self.other = self.order.send(lat.swap, part(self.up, lat, 1, False))

    def end(self):
        lat = self.lay.lat
        self.up, self.other = self.order.gate(self.up, self.other)
        up = pair(lat, part(self.up, lat, 1, True), self.other, 1)
        up = feed_columns(self.lay, up.reshape(self.lay.split, self.rows, self.columns), False)
        return up.astype(F32), self.down


class AttentionGrad:
    def __init__(self, lay, order, term):
        self.lay, self.order = lay, order
        self.terms = [term.reshape((lay.outer, 4, 4, 2) + term.shape[1:])]

    def lat(self):
        have = [None, None, None, self.lay.lat]
        self.terms, _ = shed(self.order, self.terms, self.lay.lat, have)

    def plane(self):
        self.terms = self.lay.plane.shed(self.order, self.terms, 2)

    def column(self):
        self.terms = self.lay.column.shed(self.order, self.terms, 1)

    def end(self):
        lay = self.lay
        terms = [t.reshape((2,) * len(lay.beyond) + t.shape[1:]) for t in self.terms]
        have = list(lay.beyond)
        for bit in reversed(lay.beyond):
            terms, have = shed(self.order, terms, bit, have)
        return total(terms)


def normalize(rows):
    centered = rows - jnp.mean(rows, axis=-1, keepdims=True)
    rate = lax.rsqrt(jnp.mean(centered * centered, axis=-1, keepdims=True) + 1e-05)
    return centered * rate, rate


def norm_back(grad, rows, gain):
    unit, rate = normalize(rows)
    scaled = grad * gain
    mean = jnp.mean(scaled, axis=-1, keepdims=True)
    along = jnp.mean(scaled * unit, axis=-1, keepdims=True)
    return rate * (scaled - mean - unit * along), jnp.sum(grad * unit, axis=0), jnp.sum(grad, axis=0)


def head_mask(rows, heads, width):
    row = lax.broadcasted_iota(jnp.int32, (heads * rows, width), 0) // rows
    column = lax.broadcasted_iota(jnp.int32, (heads * rows, width), 1) // (width // heads)
    return row == column


def spread_heads(rows, mask, heads):
    return jnp.where(mask, jnp.concatenate([rows] * heads, axis=0), 0)


def merge_heads(array, mask, heads):
    kept = jnp.where(mask, array, 0)
    size = array.shape[0] // heads
    total = kept[:size]
    for head in range(1, heads):
        total = total + kept[head * size : (head + 1) * size]
    return total


def slot_pairs(refs, slot, slots):
    return jnp.concatenate(
        [ref[slot * (ref.shape[0] // slots) : (slot + 1) * (ref.shape[0] // slots)] for ref in refs],
        axis=0,
    )


def soft_scores(query_wide, keys):
    scores = mm_nt(query_wide, keys)
    exponent = jnp.exp(scores - jnp.max(scores, axis=-1, keepdims=True))
    return exponent / jnp.sum(exponent, axis=-1, keepdims=True)


def attend_kernel(slots, heads, spot, refs):
    query, own_m, other_m, own_l, other_l, rows, output_w, norms, mixed, after, normed = refs
    width = query.shape[1]
    count = query.shape[0] // slots
    mask = head_mask(count, heads, width)
    for slot in range(slots):
        pairs = slot_pairs((own_m, other_m, own_l, other_l), slot, slots)
        place = slice(slot * count, (slot + 1) * count)
        wide = spread_heads(query[place] * 0.125, mask, heads)
        probs = soft_scores(wide, pairs[:, :width]).astype(BF16)
        mixed[place] = merge_heads(mm(probs, pairs[:, width:]), mask, heads).astype(BF16)
    total = rows[...] + mm(mixed[...], output_w[...])
    after[...] = total
    unit, _ = normalize(total)
    normed[...] = (unit * norms[spot[0] : spot[0] + 1] + norms[spot[1] : spot[1] + 1]).astype(BF16)


def near_memory(arrays):
    return list(arrays)


def attend(slots, heads, spot, query, own_m, other_m, own_l, other_l, rows, output_w, norms):
    shape = jax.ShapeDtypeStruct
    return pl.pallas_call(
        lambda *refs: attend_kernel(slots, heads, spot, refs),
        out_shape=(
            shape(query.shape, BF16),
            shape(rows.shape, F32),
            shape(rows.shape, BF16),
        ),
        in_specs=[pl.BlockSpec(memory_space=pltpu.VMEM)] * 8,
        out_specs=(pl.BlockSpec(memory_space=pltpu.VMEM),) * 3,
        cost_estimate=pl.CostEstimate(flops=4000000000, bytes_accessed=6000000, transcendentals=410000),
        name="attend",
    )(*near_memory((query, own_m, other_m, own_l, other_l, rows, output_w, norms)))


def attend_back_kernel(slots, heads, spot, refs):
    (
        normed_grad,
        upstream,
        after,
        query,
        own_m,
        other_m,
        own_l,
        other_l,
        mixed,
        output_w,
        norms,
        d_after,
        d_query,
        d_own_m,
        d_other_m,
        d_own_l,
        d_other_l,
        output_grad,
        norm_grad,
    ) = refs
    width = query.shape[1]
    count = query.shape[0] // slots
    mask = head_mask(count, heads, width)
    grad, d_gain, d_shift = norm_back(normed_grad[...], after[...], norms[spot : spot + 1])
    grad = grad + upstream[...]
    d_after[...] = grad
    norm_grad[...] = jnp.zeros_like(norm_grad)
    norm_grad[0:1] = d_gain[None]
    norm_grad[1:2] = d_shift[None]
    low = grad.astype(BF16)
    output_grad[...] = mm_tn(mixed[...], low).astype(BF16)
    mixed_grad = mm_nt(low, output_w[...]).astype(BF16)
    outs = (d_own_m, d_other_m, d_own_l, d_other_l)
    for slot in range(slots):
        pairs = slot_pairs((own_m, other_m, own_l, other_l), slot, slots)
        keys, values = pairs[:, :width], pairs[:, width:]
        place = slice(slot * count, (slot + 1) * count)
        wide = spread_heads(query[place] * 0.125, mask, heads)
        soft = soft_scores(wide, keys)
        wide_grad = spread_heads(mixed_grad[place], mask, heads)
        d_probs = mm_nt(wide_grad, values)
        d_values = mm_tn(soft.astype(BF16), wide_grad).astype(BF16)
        d_scores = soft * (d_probs - jnp.sum(d_probs * soft, axis=-1, keepdims=True))
        d_scores = d_scores.astype(BF16)
        d_keys = mm_tn(d_scores, wide).astype(BF16)
        d_query[place] = (merge_heads(mm(d_scores, keys), mask, heads) * 0.125).astype(BF16)
        start = 0
        for ref in outs:
            size = ref.shape[0] // slots
            ref[slot * size : (slot + 1) * size, :width] = d_keys[start : start + size]
            ref[slot * size : (slot + 1) * size, width:] = d_values[start : start + size]
            start += size


def attend_back(
    slots, heads, spot, normed_grad, upstream, after, query, pairs, mixed, output_w, norms
):
    shape = jax.ShapeDtypeStruct
    own_m, other_m, own_l, other_l = pairs
    return pl.pallas_call(
        lambda *refs: attend_back_kernel(slots, heads, spot, refs),
        out_shape=(
            shape(after.shape, F32),
            shape(query.shape, BF16),
            shape(own_m.shape, BF16),
            shape(other_m.shape, BF16),
            shape(own_l.shape, BF16),
            shape(other_l.shape, BF16),
            shape(output_w.shape, BF16),
            shape((8, after.shape[1]), F32),
        ),
        in_specs=[pl.BlockSpec(memory_space=pltpu.VMEM)] * 11,
        out_specs=(pl.BlockSpec(memory_space=pltpu.VMEM),) * 8,
        cost_estimate=pl.CostEstimate(flops=8000000000, bytes_accessed=12000000, transcendentals=410000),
        name="attend_back",
    )(
        *near_memory(
            (normed_grad, upstream, after, query)
            + (own_m, other_m, own_l, other_l, mixed, output_w, norms)
        )
    )


class Step:
    def __init__(self, lay, order, slots, media_rows, norms, level):
        self.lay, self.order, self.slots = lay, order, slots
        self.media_rows = media_rows
        self.norms = norms
        kinds = 3
        self.gains = [norms[level * kinds + k][None] for k in range(kinds)]
        self.shifts = [norms[(LAYERS + level) * kinds + k][None] for k in range(kinds)]
        self.spots = (level * kinds + 2, (LAYERS + level) * kinds + 2)

    def media(self, query_w, key_value_w, output_w):
        self.query_w, self.key_value_w, self.output_w = query_w, key_value_w, output_w
        self.heads = query_w.shape[1] // HEAD
        unit, _ = normalize(self.media_rows.astype(F32))
        self.media_norm = (unit * self.gains[0] + self.shifts[0]).astype(BF16)
        self.own_m = mm(self.media_norm, key_value_w).astype(BF16)
        self.other_m = self.order.send(self.lay.lat.swap, self.own_m)

    def latents(self, rows):
        self.rows = rows
        unit, _ = normalize(rows)
        self.latent_norm = (unit * self.gains[1] + self.shifts[1]).astype(BF16)
        self.own_l = mm(self.latent_norm, self.key_value_w).astype(BF16)
        self.other_l = self.order.send(self.lay.lat.swap, self.own_l)
        self.query = mm(self.latent_norm, self.query_w).astype(BF16)

    def attention(self):
        query, self.other_m, self.other_l = self.order.gate(self.query, self.other_m, self.other_l)
        self.mixed, self.after, self.normed = attend(
            self.slots,
            self.heads,
            self.spots,
            query,
            self.own_m,
            self.other_m,
            self.own_l,
            self.other_l,
            self.rows,
            self.output_w,
            self.norms,
        )

    def feed(self, shared, up_w, down_w):
        self.shared, self.up_w, self.down_w = shared, up_w, down_w
        shared = self.order.gate(shared)
        hidden = mm(shared, up_w)
        big = 0.5 * (1.0 + lax.erf(hidden * (2.0**-0.5)))
        density = jnp.exp(-0.5 * hidden * hidden) * ((2.0 * jnp.pi) ** -0.5)
        self.active = (hidden * big).astype(BF16)
        self.slope = (big + hidden * density).astype(BF16)
        return mm(self.active, down_w).astype(BF16)

    def feed_back(self, branch):
        branch = self.order.gate(branch)
        self.branch = branch
        self.d_hidden = (mm_nt(branch, self.down_w) * self.slope.astype(F32)).astype(BF16)
        return mm_nt(self.d_hidden, self.up_w).astype(BF16)

    def feed_terms(self):
        down = mm_tn(self.active, self.order.gate(self.branch)).astype(BF16)
        up = mm_tn(self.shared, self.d_hidden).astype(BF16)
        rows = up.shape[0] // self.lay.devices
        return FeedGrad(self.lay, self.order, up, down, rows)

    def attention_back(self, normed_grad, upstream):
        normed_grad = self.order.gate(normed_grad)
        (
            self.d_after,
            self.d_query,
            self.d_own_m,
            d_other_m,
            self.d_own_l,
            d_other_l,
            self.output_term,
            self.feed_norm,
        ) = attend_back(
            self.slots,
            self.heads,
            self.spots[0],
            normed_grad,
            upstream,
            self.after,
            self.query,
            (self.own_m, self.other_m, self.own_l, self.other_l),
            self.mixed,
            self.output_w,
            self.norms,
        )
        self.back_l = self.order.send(self.lay.lat.swap, d_other_l)
        self.back_m = self.order.send(self.lay.lat.swap, d_other_m)

    def latents_back(self):
        pairs_l = total(self.order.gate(self.d_own_l, self.back_l)).astype(BF16)
        self.pairs_l = pairs_l
        d_norm = mm_nt(pairs_l, self.key_value_w) + mm_nt(self.d_query, self.query_w)
        d_rows, self.gain_l, self.shift_l = norm_back(d_norm, self.rows, self.gains[1])
        return d_rows + self.d_after

    def right_term(self):
        lay = self.lay
        latent_norm = self.order.gate(self.latent_norm)
        width = self.output_w.shape[1]
        half = width // 2
        query = mm_tn(latent_norm, self.d_query).astype(BF16)
        query = query.reshape(lay.devices, -1, half)
        output = self.output_term.reshape(lay.devices, -1, width)
        output = jnp.concatenate([output[..., :half], output[..., half:]], axis=1)
        return AttentionGrad(lay, self.order, jnp.concatenate([query, output], axis=-1))

    def left_term(self):
        lay = self.lay
        pairs_m = total(self.order.gate(self.d_own_m, self.back_m)).astype(BF16)
        self.pairs_m = pairs_m
        term = (mm_tn(self.media_norm, pairs_m) + mm_tn(self.latent_norm, self.pairs_l)).astype(BF16)
        return AttentionGrad(lay, self.order, term.reshape(lay.devices, -1, term.shape[1]))

    def media_back(self):
        pairs_m = self.order.gate(self.pairs_m)
        d_norm = mm_nt(pairs_m, self.key_value_w)
        rows = self.media_rows.astype(F32)
        d_media, self.gain_m, self.shift_m = norm_back(d_norm, rows, self.gains[0])
        return d_media

    def norm_terms(self):
        gains = [self.gain_m, self.gain_l, self.feed_norm[0]]
        shifts = [self.shift_m, self.shift_l, self.feed_norm[1]]
        return gains, shifts


def gather_near(lay, order, rows):
    return rows, order.send(lay.tensor[0].swap, rows)


def gather_lat(lay, order, pieces):
    rows = jnp.concatenate(order.all(pieces), axis=0)
    return rows, order.send(lay.lat.swap, rows)


def return_lat(lay, order, rows):
    half = rows.shape[0] // 2
    return rows[:half], order.send(lay.lat.swap, rows[half:])


def return_near(lay, order, terms):
    half = terms[0].shape[0] // 2
    terms = order.all(terms)
    sent = total([term[half:] for term in terms]).astype(BF16)
    return [term[:half] for term in terms] + [order.send(lay.tensor[0].swap, sent)]


def make_device(lay):
    def per_device(
        media_tokens,
        image_counts,
        latent_init,
        cotangent,
        query_weight,
        key_value_weight,
        output_weight,
        up_weight,
        down_weight,
        norm_gain,
        norm_shift,
    ):
        first = norm_gain[0, :1].astype(F32)
        order = Order(first)
        slots = media_tokens.shape[0]
        model = media_tokens.shape[2]
        count = latent_init.shape[0]
        position = jnp.arange(slots) % MEDIA
        per_slot = jnp.repeat(image_counts, MEDIA)
        valid = (position < per_slot).astype(F32)[:, None, None]
        row_mask = jnp.broadcast_to(valid, (slots, count, 1)).reshape(-1, 1)
        media_rows = media_tokens.reshape(-1, model)
        device = lax.axis_index("img") * lax.axis_size("lat") + lax.axis_index("lat")
        lanes = norm_gain.shape[-1]
        kinds = norm_gain.shape[1]
        norms = jnp.concatenate(
            [norm_gain.reshape(-1, lanes), norm_shift.reshape(-1, lanes)], axis=0
        )
        spread = jnp.zeros((NORM_ROWS, model), BF16)
        spread = lax.dynamic_update_slice(spread, norms, (0, device * lanes))
        attn = [
            Attention(
                lay,
                order,
                key_value_weight[level],
                output_weight[level],
                query_weight[level],
                spread if level == 0 else None,
            )
            for level in range(LAYERS)
        ]
        feed = [Feed(lay, order, up_weight[level], down_weight[level]) for level in range(LAYERS)]
        upstream = cotangent.astype(F32).reshape(-1, model) * row_mask

        attn[0].start_column()
        feed[0].start_lat()
        feed[1].start_lat()
        feed[0].start_near()
        feed[1].start_near()
        attn[0].end_column()
        attn[0].start_plane()
        feed[0].start_far()
        attn[0].end_plane()
        attn[0].start_lat()
        feed[0].end_far()
        feed[0].start_plane()
        weights = attn[0].end_lat()
        step0 = Step(lay, order, slots, media_rows, attn[0].norms, 0)
        step0.media(*weights)
        rows0 = jnp.broadcast_to(latent_init.astype(F32), (slots, count, model)).reshape(-1, model)
        step0.latents(rows0)
        attn[1].start_column()
        feed[0].next_plane()
        attn[1].end_column()
        feed[1].start_far()
        step0.attention()
        pieces = gather_near(lay, order, step0.normed)
        pieces = gather_lat(lay, order, pieces)
        feed_w = feed[0].end_plane()
        attn[1].start_plane()
        out = step0.feed(jnp.concatenate(order.all(pieces), axis=0), *feed_w)
        terms = return_lat(lay, order, out)
        feed[1].end_far()
        terms = return_near(lay, order, terms)
        attn[1].end_plane()
        attn[1].start_lat()
        feed[1].start_plane()
        rows1 = step0.after + total(order.all(terms))
        weights = attn[1].end_lat()
        step1 = Step(lay, order, slots, media_rows, attn[0].norms, 1)
        step1.media(*weights)
        step1.latents(rows1)
        feed[1].next_plane()
        branch = gather_near(lay, order, upstream.astype(BF16))
        step1.attention()
        pieces = gather_near(lay, order, step1.normed)
        branch = gather_lat(lay, order, branch)
        pieces = gather_lat(lay, order, pieces)
        feed_w = feed[1].end_plane()
        out = step1.feed(jnp.concatenate(order.all(pieces), axis=0), *feed_w)
        terms_out = return_lat(lay, order, out)
        out = step1.feed_back(jnp.concatenate(order.all(branch), axis=0))
        terms = return_lat(lay, order, out)
        feed_grad1 = step1.feed_terms()
        terms = return_near(lay, order, terms)
        feed_grad1.plane(0)
        terms_out = return_near(lay, order, terms_out)
        step1.attention_back(total(order.all(terms)), upstream)
        upstream0 = step1.latents_back()
        branch = gather_near(lay, order, upstream0.astype(BF16))
        right1 = step1.right_term()
        right1.lat()
        left1 = step1.left_term()
        left1.lat()
        branch = gather_lat(lay, order, branch)
        feed_grad1.plane(1)
        out = step0.feed_back(jnp.concatenate(order.all(branch), axis=0))
        terms = return_lat(lay, order, out)
        feed_grad0 = step0.feed_terms()
        terms = return_near(lay, order, terms)
        feed_grad1.far()
        right1.plane()
        left1.plane()
        media1 = step1.media_back()
        step0.attention_back(total(order.all(terms)), upstream0)
        feed_grad1.start_near()
        feed_grad0.plane(0)
        last = step0.latents_back()
        right0 = step0.right_term()
        right0.lat()
        left0 = step0.left_term()
        left0.lat()
        right1.column()
        left1.column()
        feed_grad1.start_lat()
        feed_grad0.plane(1)
        right0.plane()
        left0.plane()
        media_grad = media1 + step0.media_back()
        gains0, shifts0 = step0.norm_terms()
        gains1, shifts1 = step1.norm_terms()
        small = jnp.stack(gains0 + gains1 + shifts0 + shifts1)
        small = jnp.pad(small, ((0, NORM_ROWS - small.shape[0]), (0, 0)))
        latent = jnp.sum(last.reshape(slots, count, model), axis=0)
        tail = jnp.concatenate([latent, small], axis=0)
        for bit in lay.img[:2]:
            tail = tail + order.send(bit.swap, tail)
        feed_grad0.far()
        right0.column()
        left0.column()
        for bit in lay.img[2:]:
            tail = tail + order.send(bit.swap, tail)
        feed_grad0.start_near()
        feed_grad0.start_lat()
        small = tail[count:]
        small = small + order.send(lay.lat.swap, small)
        small = lax.dynamic_slice(small, (0, device * lanes), (2 * LAYERS * kinds, lanes))
        small = small + (order.token - first)
        small = small.reshape(2, LAYERS, kinds, lanes)
        rights = [right0.end(), right1.end()]
        lefts = [left0.end(), left1.end()]
        feeds = [feed_grad0.end(), feed_grad1.end()]
        half = model // 2
        outs = []
        for right in rights:
            cut = right.shape[0] // 2
            outs.append(jnp.concatenate([right[:cut, half:], right[cut:, half:]], axis=1))
        resampled = ((step1.after + total(terms_out)) * row_mask).reshape(cotangent.shape)
        return (
            resampled,
            media_grad.reshape(media_tokens.shape),
            tail[:count],
            jnp.stack([right[:, :half] for right in rights]),
            jnp.stack(lefts),
            jnp.stack(outs),
            jnp.stack([entry[0] for entry in feeds]),
            jnp.stack([entry[1] for entry in feeds]),
            small[0],
            small[1],
        )

    return per_device


def solution(mesh):
    lay = Layout(mesh.shape["img"], mesh.shape["lat"])
    in_specs = (
        P("img", "lat", None),
        P("img"),
        P("lat", None),
        P("img", "lat", None),
        P(None, ("img", "lat"), None),
        P(None, ("img", "lat"), None),
        P(None, ("img", "lat"), None),
        P(None, ("img", "lat"), None),
        P(None, ("img", "lat"), None),
        P(None, None, ("img", "lat")),
        P(None, None, ("img", "lat")),
    )
    out_specs = (
        P("img", "lat", None),
        P("img", "lat", None),
        P("lat", None),
        P(None, ("img", "lat"), None),
        P(None, ("img", "lat"), None),
        P(None, ("img", "lat"), None),
        P(None, ("img", "lat"), None),
        P(None, ("img", "lat"), None),
        P(None, None, ("img", "lat")),
        P(None, None, ("img", "lat")),
    )
    return jax.shard_map(
        make_device(lay), mesh=mesh, in_specs=in_specs, out_specs=out_specs, check_vma=False
    )
```

time: 671 us -> 533 us (0.79)
  waiting for transfers between devices: 259 us -> 178 us
  local copies, waits for them, and re-layouts: 145 us -> 70.4 us
  Pallas kernels: 0 us -> 35.2 us
  matrix products: 82.3 us -> 52.2 us
  starting transfers between devices: 72 us -> 96.4 us
  other arithmetic: 95.7 us -> 85.1 us
    ppermute x89 -> x63, waiting for transfers between devices: 259 us -> 86 us  [swap(): return lax.ppermute(array, self.axis, self.pairs)]
    ppermute x0 -> x36, waiting for transfers between devices: none -> 92.1 us  [_swap(): return lambda array: lax.ppermute(array, 'img', pairs)]
    concatenate x8 -> x10, local copies, waits for them, and re-layouts: 61.5 us -> 4.48 us  [the longest x4 3.32 us: end_lat(): jnp.concatenate([a[..., rows:middle, half:], a[..., middle:2 * rows, half...]
    ppermute x0 -> x36, starting transfers between devices: none -> 48.6 us  [_swap(): return lambda array: lax.ppermute(array, 'img', pairs)]
    pallas_call x0 -> x4, Pallas kernels: none -> 35.2 us  [the longest x2 21.9 us: attend_back(): pl.pallas_call(lambda *refs: attend_back_kernel(slots, heads, spot, refs)...]
    ppermute x89 -> x63, starting transfers between devices: 72 us -> 47.8 us  [swap(): return lax.ppermute(array, self.axis, self.pairs)]
    dot_general x12 -> x0, matrix products: 21.8 us -> none  [the longest x2 5.57 us: layer_backward(): jnp.einsum('shqk,sqhe->skhe', probs, mixed_grad, preferred_element_type=F32)]
    squeeze x9 -> x31, local copies, waits for them, and re-layouts: 4.74 us -> 21.9 us  [the longest x28 18.7 us: pick(): return lax.dynamic_index_in_dim(array, index, axis, keepdims=False)]
  transfers between devices with their start and end apart: 89 -> 99, of which waited for: 37 -> 30; matrix products, arithmetic and copies ran while one was open for 41% -> 33% of each run, Pallas kernels for 0% -> 7%
where the time goes in v2:
time: 533 us; the launch traced here: 522 us
  waiting for transfers between devices  178 us (33%)
  starting transfers between devices  96.4 us (18%)
  other arithmetic  85.1 us (16%)
  local copies, waits for them, and re-layouts  70.4 us (13%)
  matrix products  52.2 us (10%)
  Pallas kernels  35.2 us (7%)
    ppermute x36, waiting for transfers between devices, _swap(): return lambda array: lax.ppermute(array, 'img', pairs)  92.1 us
    ppermute x63, waiting for transfers between devices, swap(): return lax.ppermute(array, self.axis, self.pairs)  86 us
    ppermute x36, starting transfers between devices, _swap(): return lambda array: lax.ppermute(array, 'img', pairs)  48.6 us
    ppermute x63, starting transfers between devices, swap(): return lax.ppermute(array, self.axis, self.pairs)  47.8 us
    pallas_call x2, Pallas kernels, attend_back(): pl.pallas_call(lambda *refs: attend_back_kernel(slots, heads, spot, refs)...  21.9 us
    dot_general x10, matrix products, mm_nt(): lax.dot_general(a, b, (((1,), (1,)), ((), ())), preferred_element_type=F32)  20.4 us
    another operation x46, other arithmetic, pair(): jnp.stack([jnp.where(low, own, other), jnp.where(low, other, own)], axis=...  19.9 us
    squeeze x28, local copies, waits for them, and re-layouts, pick(): return lax.dynamic_index_in_dim(array, index, axis, keepdims=False)  18.7 us
  transfers between devices with their start and end apart: 99, of which 30 were waited for; matrix products, arithmetic and copies ran while one was open for 33% of the time, Pallas kernels for 7%

profile of v2, /device:TPU:0, one launch (start us, length us, event | category | flops | bytes accessed | tf_op | source)
XLA Modules:
  0.0 522.1 jit_solution(264722698981647461)
XLA Ops:
  7.9 3.1 collective-permute-start
  18.9 7.2 %collective-permute-done.1 = bf16[1,80,1024]{2,1,0:T(8,128)(2,1)S(1)} collective-permute-done((bf16[1,80,1024]{2,1,0:T(8,128)(2,1)S(1)}, bf16[1,80,1024]{2,1,0:T(8,128)(2,1)S(1)}, u32[]{:S(2)}, u32[]{:S(2)}) %collective-permute-start.1) | collective-permute-done | bytes 163872 | tf_op jit(solution)/shard_map/ppermute | solution.py:55
  31.6 12.3 %collective-permute-done.5 = bf16[1,4,80,1024]{3,2,1,0:T(8,128)(2,1)S(1)} collective-permute-done((bf16[1,4,80,1024]{3,2,1,0:T(8,128)(2,1)S(1)}, bf16[1,4,80,1024]{3,2,1,0:T(8,128)(2,1)S(1)}, u32[]{:S(2)}, u32[]{:S(2)}) %collective-permute-start.5) | collective-permute-done | bytes 655392 | tf_op jit(solution)/shard_map/ppermute | solution.py:55
  43.9 11.0 %collective-permute-done.6 = bf16[1,4,80,1024]{3,2,1,0:T(8,128)(2,1)S(1)} collective-permute-done((bf16[1,4,80,1024]{3,2,1,0:T(8,128)(2,1)S(1)}, bf16[1,4,80,1024]{3,2,1,0:T(8,128)(2,1)S(1)}, u32[]{:S(2)}, u32[]{:S(2)}) %collective-permute-start.6) | collective-permute-done | bytes 655392 | tf_op jit(solution)/shard_map/ppermute | solution.py:55
  60.5 5.1 collective-permute-start.10
  66.7 22.7 %collective-permute-done.10 = bf16[256,1024]{1,0:T(8,128)(2,1)S(1)} collective-permute-done((bf16[256,1024]{1,0:T(8,128)(2,1)S(1)}, bf16[256,1024]{1,0:T(8,128)(2,1)S(1)}, u32[]{:S(2)}, u32[]{:S(2)}) %collective-permute-start.10) | collective-permute-done | bytes 524320 | tf_op jit(solution)/shard_map/ppermute | solution.py:45
  112.2 4.4 collective-permute-done.15
  121.0 6.7 %attend.2 = (bf16[160,512]{1,0:T(8,128)(2,1)}, f32[160,1024]{1,0:T(8,128)}, bf16[160,1024]{1,0:T(8,128)(2,1)}) custom-call(bf16[160,512]{1,0:T(8,128)(2,1)} %convolution_convert_fusion.15.refs_0_.refs_3_, bf16[640,1024]{1,0:T(8,128)(2,1)} %copy-done.119, bf16[640,1024]{1,0:T(8,128)(2,1)} %copy-done.120, bf16[160,1024]{1,0:T(8,128)(2,1)} %copy-done.85, ...), custom_call_target="tpu_custom_call" | custom-call | flops 4000000000 | bytes 6000000 | tf_op jit(solution)/shard_map/attend/pallas_call | solution.py:452
  131.1 6.4 %collective-permute-done.19 = bf16[160,1024]{1,0:T(8,128)(2,1)S(1)} collective-permute-done((bf16[160,1024]{1,0:T(8,128)(2,1)}, bf16[160,1024]{1,0:T(8,128)(2,1)S(1)}, u32[]{:S(2)}, u32[]{:S(2)}) %collective-permute-start.19) | collective-permute-done | bytes 327712 | tf_op jit(solution)/shard_map/ppermute | solution.py:45
  137.7 3.2 collective-permute-done.21
  146.3 2.9 multiply_convert_fusion.3
  157.8 19.7 %collective-permute-done.24 = bf16[256,1024]{1,0:T(8,128)(2,1)S(1)} collective-permute-done((bf16[256,1024]{1,0:T(8,128)(2,1)S(1)}, bf16[256,1024]{1,0:T(8,128)(2,1)S(1)}, u32[]{:S(2)}, u32[]{:S(2)}) %collective-permute-start.24) | collective-permute-done | bytes 524320 | tf_op jit(solution)/shard_map/ppermute | solution.py:45
  187.3 6.5 %collective-permute-done.25 = bf16[160,1024]{1,0:T(8,128)(2,1)S(1)} collective-permute-done((bf16[160,1024]{1,0:T(8,128)(2,1)}, bf16[160,1024]{1,0:T(8,128)(2,1)S(1)}, u32[]{:S(2)}, u32[]{:S(2)}) %collective-permute-start.25) | collective-permute-done | bytes 327712 | tf_op jit(solution)/shard_map/ppermute | solution.py:45
  213.3 6.6 %attend.3 = (bf16[160,512]{1,0:T(8,128)(2,1)}, f32[160,1024]{1,0:T(8,128)}, bf16[160,1024]{1,0:T(8,128)(2,1)}) custom-call(bf16[160,512]{1,0:T(8,128)(2,1)} %convolution_convert_fusion.14.refs_0_.refs_3_, bf16[640,1024]{1,0:T(8,128)(2,1)} %copy-done.121, bf16[640,1024]{1,0:T(8,128)(2,1)} %copy-done.122, bf16[160,1024]{1,0:T(8,128)(2,1)} %copy-done.86, ...), custom_call_target="tpu_custom_call" | custom-call | flops 4000000000 | bytes 6000000 | tf_op jit(solution)/shard_map/attend/pallas_call | solution.py:452
  228.5 4.7 collective-permute-done.37
  259.2 3.1 collective-permute-done.43
  263.3 10.8 %attend_back.2 = (f32[160,1024]{1,0:T(8,128)}, bf16[160,512]{1,0:T(8,128)(2,1)}, bf16[640,1024]{1,0:T(8,128)(2,1)}, bf16[640,1024]{1,0:T(8,128)(2,1)}, bf16[160,...) custom-call(f32[160,1024]{1,0:T(8,128)} %convert_add_fusion.3.refs_0_, ...), custom_call_target="tpu_custom_call" | custom-call | flops 8000000000 | bytes 12000000 | tf_op jit(solution)/shard_map/attend_back/pallas_call | solution.py:527
  291.3 3.8 collective-permute-done.49
  309.3 3.2 convolution_convert_fusion
  312.5 3.2 convolution_convert_fusion.1
  331.8 3.1 fusion.101
  334.9 6.8 %collective-permute-done.55 = bf16[160,1024]{1,0:T(8,128)(2,1)S(1)} collective-permute-done((bf16[160,1024]{1,0:T(8,128)(2,1)S(1)}, bf16[160,1024]{1,0:T(8,128)(2,1)S(1)}, u32[]{:S(2)}, u32[]{:S(2)}) %collective-permute-start.55) | collective-permute-done | bytes 327712 | tf_op jit(solution)/shard_map/ppermute | solution.py:45
  344.0 11.1 %attend_back.3 = (f32[160,1024]{1,0:T(8,128)}, bf16[160,512]{1,0:T(8,128)(2,1)}, bf16[640,1024]{1,0:T(8,128)(2,1)}, bf16[640,1024]{1,0:T(8,128)(2,1)}, bf16[160,...) custom-call(f32[160,1024]{1,0:T(8,128)} %convert_add_fusion.2.refs_0_, ...), custom_call_target="tpu_custom_call" | custom-call | flops 8000000000 | bytes 12000000 | tf_op jit(solution)/shard_map/attend_back/pallas_call | solution.py:527
  388.1 24.7 %collective-permute-done.65 = bf16[1,4,32,1024]{3,2,1,0:T(8,128)(2,1)S(1)} collective-permute-done((bf16[1,4,32,1024]{3,2,1,0:T(8,128)(2,1)S(1)}, bf16[1,4,32,1024]{3,2,1,0:T(8,128)(2,1)S(1)}, u32[]{:S(2)}, u32[]{:S(2)}) %collective-permute-start.65) | collective-permute-done | bytes 262176 | tf_op jit(solution)/shard_map/ppermute | solution.py:55
  419.8 2.9 collective-permute-start.85
  430.1 2.9 collective-permute-start.91
  443.2 4.7 multiply_reduce_fusion.1
  450.9 5.3 %add_multiply_fusion = f32[640,1024]{1,0:T(8,128)} fusion(f32[640,1024]{1,0:T(8,128)} %get-tuple-element.1250, f32[640,1024]{1,0:T(8,128)} %fusion.101, bf16[5,128,1024]{2,1,0:T(8,128)(2,1)S(1)} %copy-done, f32[640]{0:T(1024)S(1)} %broadcast_multiply_fusion, f32[640]{0:T(1024)S(1)} %broadcast_multiply_fusion.1, f32[1024]{0:T(1024)S(1)} %bitcast.788, ...), kind=kLoop, calls=%fused_computation.17 | loop fusion | flops 8519680 | bytes 9198592 | tf_op jit(solution)/shard_map/add | solution.py:831
  463.9 4.6 collective-permute-done.77
  477.1 7.6 %collective-permute-done.83 = bf16[1,32,1024]{2,1,0:T(8,128)(2,1)S(1)} collective-permute-done((bf16[1,32,1024]{2,1,0:T(8,128)(2,1)S(1)}, bf16[1,32,1024]{2,1,0:T(8,128)(2,1)S(1)}, u32[]{:S(2)}, u32[]{:S(2)}) %collective-permute-start.83) | collective-permute-done | bytes 65568 | tf_op jit(solution)/shard_map/ppermute | solution.py:55
  495.1 13.3 %collective-permute-done.89 = bf16[1,32,1024]{2,1,0:T(8,128)(2,1)S(1)} collective-permute-done((bf16[1,32,1024]{2,1,0:T(8,128)(2,1)S(1)}, bf16[1,32,1024]{2,1,0:T(8,128)(2,1)S(1)}, u32[]{:S(2)}, u32[]{:S(2)}) %collective-permute-start.89) | collective-permute-done | bytes 65568 | tf_op jit(solution)/shard_map/ppermute | solution.py:55
  512.2 4.5 collective-permute-done.81
  (820 shorter events, 278.9 us)
Async XLA Ops:
  28.1 26.8 %collective-permute-start.6 = (bf16[1,4,80,1024]{3,2,1,0:T(8,128)(2,1)S(1)}, bf16[1,4,80,1024]{3,2,1,0:T(8,128)(2,1)S(1)}, u32[]{:S(2)}, u32[]{:S(2)}) collective-permute-start(bf16[1,4,80,1024]{3,2,1,0:T(8,128)(2,1)S(1)} %pad_maximum_fusion.29), channel_id=1, source_target_pairs={{0,4},{2,6},{4,0},{6,2},{8,12},{10,14},{12,8},{14,10},{16,20},{18,... | collective-permute-start | bytes 1966088 | tf_op jit(solution)/shard_map/ppermute | solution.py:55
  29.6 26.4 %collective-permute-start.7 = (bf16[1,4,80,1024]{3,2,1,0:T(8,128)(2,1)S(1)}, bf16[1,4,80,1024]{3,2,1,0:T(8,128)(2,1)}, u32[]{:S(2)}, u32[]{:S(2)}) collective-permute-start(bf16[1,4,80,1024]{3,2,1,0:T(8,128)(2,1)S(1)} %pad_maximum_fusion.29), channel_id=1, source_target_pairs={{0,6},{2,4},{4,2},{6,0},{8,14},{10,12},{12,10},{14,8},{16,22},{18,... | collective-permute-start | bytes 1966088 | tf_op jit(solution)/shard_map/ppermute | solution.py:55
  59.2 32.6 %collective-permute-start.9 = (bf16[1,4,4,80,1024]{4,3,2,1,0:T(8,128)(2,1)}, bf16[1,4,4,80,1024]{4,3,2,1,0:T(8,128)(2,1)}, u32[]{:S(2)}, u32[]{:S(2)}) collective-permute-start(bf16[1,4,4,80,1024]{4,3,2,1,0:T(8,128)(2,1)} %pad_maximum_fusion), channel_id=1, source_target_pairs={{0,1},{1,0},{2,3},{3,2},{4,5},{5,4},{6,7},{7,6},{8,9},{9,8},{10,11... | collective-permute-start | bytes 7864328 | tf_op jit(solution)/shard_map/ppermute | solution.py:45
  60.5 28.9 %collective-permute-start.10 = (bf16[256,1024]{1,0:T(8,128)(2,1)S(1)}, bf16[256,1024]{1,0:T(8,128)(2,1)S(1)}, u32[]{:S(2)}, u32[]{:S(2)}) collective-permute-start(bf16[256,1024]{1,0:T(8,128)(2,1)S(1)} %pad_maximum_fusion.32), channel_id=1, source_target_pairs={{0,16},{2,18},{4,20},{6,22},{8,24},{10,26},{12,28},{14,30},{16,0},... | collective-permute-start | bytes 1572872 | tf_op jit(solution)/shard_map/ppermute | solution.py:45
  66.7 51.9 %collective-permute-start.13 = (bf16[2,32,1024]{2,1,0:T(8,128)(2,1)}, bf16[2,32,1024]{2,1,0:T(8,128)(2,1)S(1)}, u32[]{:S(2)}, u32[]{:S(2)}) collective-permute-start(bf16[2,32,1024]{2,1,0:T(8,128)(2,1)} %fusion.40), channel_id=1, source_target_pairs={{0,8},{2,10},{4,12},{6,14},{8,0},{10,2},{12,4},{14,6},{16,24},{18,... | collective-permute-start | bytes 393224 | tf_op jit(solution)/shard_map/ppermute | solution.py:45
  116.6 24.3 %collective-permute-start.21 = (bf16[2,2,2,2,32,1024]{5,4,3,2,1,0:T(8,128)(2,1)S(1)}, bf16[2,2,2,2,32,1024]{5,4,3,2,1,0:T(8,128)(2,1)}, u32[]{:S(2)}, u32[]{:S(2)}) collective-permute-start(bf16[2,2,2,2,32,1024]{5,4,3,2,1,0:T(8,128)(2,1)S(1)} %pad_maximum_fusion.14), channel_id=1, source_target_pairs={{0,4},{2,6},{4,0},{6,2},{8,12},{10,14},{12,8},{14,10},{16,20},{18,... | collective-permute-start | bytes 3145736 | tf_op jit(solution)/shard_map/ppermute | solution.py:45
  150.9 26.5 %collective-permute-start.23 = (bf16[320,1024]{1,0:T(8,128)(2,1)S(1)}, bf16[320,1024]{1,0:T(8,128)(2,1)S(1)}, u32[]{:S(2)}, u32[]{:S(2)}) collective-permute-start(bf16[320,1024]{1,0:T(8,128)(2,1)S(1)} %get-tuple-element.599), channel_id=1, source_target_pairs={{0,1},{1,0},{2,3},{3,2},{4,5},{5,4},{6,7},{7,6},{8,9},{9,8},{10,11... | collective-permute-start | bytes 1966088 | tf_op jit(solution)/shard_map/ppermute | solution.py:45
  151.9 25.6 %collective-permute-start.24 = (bf16[256,1024]{1,0:T(8,128)(2,1)S(1)}, bf16[256,1024]{1,0:T(8,128)(2,1)S(1)}, u32[]{:S(2)}, u32[]{:S(2)}) collective-permute-start(bf16[256,1024]{1,0:T(8,128)(2,1)S(1)} %copy-done.30), channel_id=1, source_target_pairs={{0,16},{2,18},{4,20},{6,22},{8,24},{10,26},{12,28},{14,30},{16,0},... | collective-permute-start | bytes 1572872 | tf_op jit(solution)/shard_map/ppermute | solution.py:45
  154.3 24.1 %collective-permute-start.26 = (bf16[1,4,64,1024]{3,2,1,0:T(8,128)(2,1)S(1)}, bf16[1,4,64,1024]{3,2,1,0:T(8,128)(2,1)S(1)}, u32[]{:S(2)}, u32[]{:S(2)}) collective-permute-start(bf16[1,4,64,1024]{3,2,1,0:T(8,128)(2,1)S(1)} %pad_maximum_fusion.36), channel_id=1, source_target_pairs={{0,2},{2,0},{4,6},{6,4},{8,10},{10,8},{12,14},{14,12},{16,18},{18,... | collective-permute-start | bytes 1572872 | tf_op jit(solution)/shard_map/ppermute | solution.py:55
  208.6 24.6 %collective-permute-start.37 = (bf16[2,2,2,2,32,1024]{5,4,3,2,1,0:T(8,128)(2,1)}, bf16[2,2,2,2,32,1024]{5,4,3,2,1,0:T(8,128)(2,1)}, u32[]{:S(2)}, u32[]{:S(2)}) collective-permute-start(bf16[2,2,2,2,32,1024]{5,4,3,2,1,0:T(8,128)(2,1)} %pad_maximum_fusion.18), channel_id=1, source_target_pairs={{0,4},{2,6},{4,0},{6,2},{8,12},{10,14},{12,8},{14,10},{16,20},{18,... | collective-permute-start | bytes 3145736 | tf_op jit(solution)/shard_map/ppermute | solution.py:45
  209.2 24.3 %collective-permute-start.38 = (bf16[2,2,128,1024]{3,2,1,0:T(8,128)(2,1)}, bf16[2,2,128,1024]{3,2,1,0:T(8,128)(2,1)}, u32[]{:S(2)}, u32[]{:S(2)}) collective-permute-start(bf16[2,2,128,1024]{3,2,1,0:T(8,128)(2,1)} %pad_maximum_fusion.17), channel_id=1, source_target_pairs={{0,2},{2,0},{4,6},{6,4},{8,10},{10,8},{12,14},{14,12},{16,18},{18,... | collective-permute-start | bytes 3145736 | tf_op jit(solution)/shard_map/ppermute | solution.py:45
  256.0 39.1 %collective-permute-start.48 = (bf16[2,2,2,2,32,1024]{5,4,3,2,1,0:T(8,128)(2,1)}, bf16[2,2,2,2,32,1024]{5,4,3,2,1,0:T(8,128)(2,1)}, u32[]{:S(2)}, u32[]{:S(2)}) collective-permute-start(bf16[2,2,2,2,32,1024]{5,4,3,2,1,0:T(8,128)(2,1)} %get-tuple-element.735), channel_id=1, source_target_pairs={{0,4},{2,6},{4,0},{6,2},{8,12},{10,14},{12,8},{14,10},{16,20},{18,... | collective-permute-start | bytes 3145736 | tf_op jit(solution)/shard_map/ppermute | solution.py:45
  258.5 39.3 %collective-permute-start.51 = (bf16[2,2,128,1024]{3,2,0,1:T(8,128)(2,1)}, bf16[2,2,128,1024]{3,2,0,1:T(8,128)(2,1)}, u32[]{:S(2)}, u32[]{:S(2)}) collective-permute-start(bf16[2,2,128,1024]{3,2,0,1:T(8,128)(2,1)} %bitcast.620), channel_id=1, source_target_pairs={{0,2},{2,0},{4,6},{6,4},{8,10},{10,8},{12,14},{14,12},{16,18},{18,... | collective-permute-start | bytes 3145736 | tf_op jit(solution)/shard_map/ppermute | solution.py:45
  284.9 33.0 %collective-permute-start.47 = (bf16[1,4,4,32,1024]{4,3,1,2,0:T(8,128)(2,1)S(1)}, bf16[1,4,4,32,1024]{4,3,1,2,0:T(8,128)(2,1)S(1)}, u32[]{:S(2)}, u32[]{:S(2)}) collective-permute-start(bf16[1,4,4,32,1024]{4,3,1,2,0:T(8,128)(2,1)S(1)} %bitcast.751), channel_id=1, source_target_pairs={{0,1},{1,0},{2,3},{3,2},{4,5},{5,4},{6,7},{7,6},{8,9},{9,8},{10,11... | collective-permute-start | bytes 3145736 | tf_op jit(solution)/shard_map/ppermute | solution.py:45
  291.1 30.4 %collective-permute-start.46 = (bf16[1,4,4,32,1024]{4,3,1,2,0:T(8,128)(2,1)S(1)}, bf16[1,4,4,32,1024]{4,3,1,2,0:T(8,128)(2,1)S(1)}, u32[]{:S(2)}, u32[]{:S(2)}) collective-permute-start(bf16[1,4,4,32,1024]{4,3,1,2,0:T(8,128)(2,1)S(1)} %bitcast.752), channel_id=1, source_target_pairs={{0,1},{1,0},{2,3},{3,2},{4,5},{5,4},{6,7},{7,6},{8,9},{9,8},{10,11... | collective-permute-start | bytes 3145736 | tf_op jit(solution)/shard_map/ppermute | solution.py:45
  327.0 31.2 %collective-permute-start.58 = (bf16[256,1024]{1,0:T(8,128)(2,1)}, bf16[256,1024]{1,0:T(8,128)(2,1)}, u32[]{:S(2)}, u32[]{:S(2)}) collective-permute-start(bf16[256,1024]{1,0:T(8,128)(2,1)} %fusion.17), channel_id=1, source_target_pairs={{0,16},{2,18},{4,20},{6,22},{8,24},{10,26},{12,28},{14,30},{16,0},... | collective-permute-start | bytes 1572872 | tf_op jit(solution)/shard_map/ppermute | solution.py:45
  328.6 57.2 %collective-permute-start.64 = (bf16[1,4,32,1024]{3,2,1,0:T(8,128)(2,1)}, bf16[1,4,32,1024]{3,2,1,0:T(8,128)(2,1)}, u32[]{:S(2)}, u32[]{:S(2)}) collective-permute-start(bf16[1,4,32,1024]{3,2,1,0:T(8,128)(2,1)} %get-tuple-element.842), channel_id=1, source_target_pairs={{0,2},{2,0},{4,6},{6,4},{8,10},{10,8},{12,14},{14,12},{16,18},{18,... | collective-permute-start | bytes 786440 | tf_op jit(solution)/shard_map/ppermute | solution.py:55
  329.9 51.9 %collective-permute-start.67 = (bf16[1,4,32,1024]{3,2,1,0:T(8,128)(2,1)}, bf16[1,4,32,1024]{3,2,1,0:T(8,128)(2,1)}, u32[]{:S(2)}, u32[]{:S(2)}) collective-permute-start(bf16[1,4,32,1024]{3,2,1,0:T(8,128)(2,1)} %get-tuple-element.845), channel_id=1, source_target_pairs={{0,2},{2,0},{4,6},{6,4},{8,10},{10,8},{12,14},{14,12},{16,18},{18,... | collective-permute-start | bytes 786440 | tf_op jit(solution)/shard_map/ppermute | solution.py:55
  330.6 51.9 %collective-permute-start.68 = (bf16[1,4,32,1024]{3,2,1,0:T(8,128)(2,1)}, bf16[1,4,32,1024]{3,2,1,0:T(8,128)(2,1)}, u32[]{:S(2)}, u32[]{:S(2)}) collective-permute-start(bf16[1,4,32,1024]{3,2,1,0:T(8,128)(2,1)} %get-tuple-element.846), channel_id=1, source_target_pairs={{0,4},{2,6},{4,0},{6,2},{8,12},{10,14},{12,8},{14,10},{16,20},{18,... | collective-permute-start | bytes 786440 | tf_op jit(solution)/shard_map/ppermute | solution.py:55
  341.6 42.4 %collective-permute-start.69 = (bf16[1,4,32,1024]{3,2,1,0:T(8,128)(2,1)}, bf16[1,4,32,1024]{3,2,1,0:T(8,128)(2,1)}, u32[]{:S(2)}, u32[]{:S(2)}) collective-permute-start(bf16[1,4,32,1024]{3,2,1,0:T(8,128)(2,1)} %get-tuple-element.847), channel_id=1, source_target_pairs={{0,6},{2,4},{4,2},{6,0},{8,14},{10,12},{12,10},{14,8},{16,22},{18,... | collective-permute-start | bytes 786440 | tf_op jit(solution)/shard_map/ppermute | solution.py:55
  376.4 38.1 %collective-permute-start.62 = (bf16[2,2,2,2,32,1024]{5,4,3,2,1,0:T(8,128)(2,1)S(1)}, bf16[2,2,2,2,32,1024]{5,4,3,2,1,0:T(8,128)(2,1)S(1)}, u32[]{:S(2)}, u32[]{:S(2)}) collective-permute-start(bf16[2,2,2,2,32,1024]{5,4,3,2,1,0:T(8,128)(2,1)S(1)} %copy-done.54), channel_id=1, source_target_pairs={{0,4},{2,6},{4,0},{6,2},{8,12},{10,14},{12,8},{14,10},{16,20},{18,... | collective-permute-start | bytes 3145736 | tf_op jit(solution)/shard_map/ppermute | solution.py:45
  381.8 31.0 %collective-permute-start.65 = (bf16[1,4,32,1024]{3,2,1,0:T(8,128)(2,1)S(1)}, bf16[1,4,32,1024]{3,2,1,0:T(8,128)(2,1)S(1)}, u32[]{:S(2)}, u32[]{:S(2)}) collective-permute-start(bf16[1,4,32,1024]{3,2,1,0:T(8,128)(2,1)S(1)} %copy-done.91), channel_id=1, source_target_pairs={{0,4},{2,6},{4,0},{6,2},{8,12},{10,14},{12,8},{14,10},{16,20},{18,... | collective-permute-start | bytes 786440 | tf_op jit(solution)/shard_map/ppermute | solution.py:55
  382.5 30.4 %collective-permute-start.66 = (bf16[1,4,32,1024]{3,2,1,0:T(8,128)(2,1)S(1)}, bf16[1,4,32,1024]{3,2,1,0:T(8,128)(2,1)S(1)}, u32[]{:S(2)}, u32[]{:S(2)}) collective-permute-start(bf16[1,4,32,1024]{3,2,1,0:T(8,128)(2,1)S(1)} %copy-done.90), channel_id=1, source_target_pairs={{0,6},{2,4},{4,2},{6,0},{8,14},{10,12},{12,10},{14,8},{16,22},{18,... | collective-permute-start | bytes 786440 | tf_op jit(solution)/shard_map/ppermute | solution.py:55
  384.0 33.3 %collective-permute-start.61 = (bf16[2,2,128,1024]{3,2,0,1:T(8,128)(2,1)S(1)}, bf16[2,2,128,1024]{3,2,0,1:T(8,128)(2,1)S(1)}, u32[]{:S(2)}, u32[]{:S(2)}) collective-permute-start(bf16[2,2,128,1024]{3,2,0,1:T(8,128)(2,1)S(1)} %bitcast.750), channel_id=1, source_target_pairs={{0,2},{2,0},{4,6},{6,4},{8,10},{10,8},{12,14},{14,12},{16,18},{18,... | collective-permute-start | bytes 3145736 | tf_op jit(solution)/shard_map/ppermute | solution.py:45
  386.5 27.9 %collective-permute-start.63 = (bf16[2,32,1024]{2,1,0:T(8,128)(2,1)S(1)}, bf16[2,32,1024]{2,1,0:T(8,128)(2,1)S(1)}, u32[]{:S(2)}, u32[]{:S(2)}) collective-permute-start(bf16[2,32,1024]{2,1,0:T(8,128)(2,1)S(1)} %copy-done.102), channel_id=1, source_target_pairs={{0,8},{2,10},{4,12},{6,14},{8,0},{10,2},{12,4},{14,6},{16,24},{18,... | collective-permute-start | bytes 393224 | tf_op jit(solution)/shard_map/ppermute | solution.py:45
  412.8 29.1 %collective-permute-start.59 = (bf16[1,4,4,32,1024]{4,3,1,2,0:T(8,128)(2,1)S(1)}, bf16[1,4,4,32,1024]{4,3,1,2,0:T(8,128)(2,1)S(1)}, u32[]{:S(2)}, u32[]{:S(2)}) collective-permute-start(bf16[1,4,4,32,1024]{4,3,1,2,0:T(8,128)(2,1)S(1)} %bitcast.746), channel_id=1, source_target_pairs={{0,1},{1,0},{2,3},{3,2},{4,5},{5,4},{6,7},{7,6},{8,9},{9,8},{10,11... | collective-permute-start | bytes 3145736 | tf_op jit(solution)/shard_map/ppermute | solution.py:45
  425.1 34.6 %collective-permute-start.78 = (bf16[2,2,2,32,1024]{4,3,2,1,0:T(8,128)(2,1)}, bf16[2,2,2,32,1024]{4,3,2,1,0:T(8,128)(2,1)}, u32[]{:S(2)}, u32[]{:S(2)}) collective-permute-start(bf16[2,2,2,32,1024]{4,3,2,1,0:T(8,128)(2,1)} %fusion.18), channel_id=1, source_target_pairs={{0,2},{2,0},{4,6},{6,4},{8,10},{10,8},{12,14},{14,12},{16,18},{18,... | collective-permute-start | bytes 1572872 | tf_op jit(solution)/shard_map/ppermute | solution.py:45
  434.8 25.8 %collective-permute-start.79 = (bf16[2,128,1024]{2,1,0:T(8,128)(2,1)}, bf16[2,128,1024]{2,1,0:T(8,128)(2,1)}, u32[]{:S(2)}, u32[]{:S(2)}) collective-permute-start(bf16[2,128,1024]{2,1,0:T(8,128)(2,1)} %fusion.19), channel_id=1, source_target_pairs={{0,4},{2,6},{4,0},{6,2},{8,12},{10,14},{12,8},{14,10},{16,20},{18,... | collective-permute-start | bytes 1572872 | tf_op jit(solution)/shard_map/ppermute | solution.py:45
  436.3 27.6 %collective-permute-start.75 = (bf16[1,4,32,1024]{3,2,1,0:T(8,128)(2,1)}, bf16[1,4,32,1024]{3,2,1,0:T(8,128)(2,1)}, u32[]{:S(2)}, u32[]{:S(2)}) collective-permute-start(bf16[1,4,32,1024]{3,2,1,0:T(8,128)(2,1)} %get-tuple-element.902), channel_id=1, source_target_pairs={{0,2},{2,0},{4,6},{6,4},{8,10},{10,8},{12,14},{14,12},{16,18},{18,... | collective-permute-start | bytes 786440 | tf_op jit(solution)/shard_map/ppermute | solution.py:55
  459.7 26.7 %collective-permute-start.72 = (bf16[1,4,32,1024]{3,2,1,0:T(8,128)(2,1)S(1)}, bf16[1,4,32,1024]{3,2,1,0:T(8,128)(2,1)S(1)}, u32[]{:S(2)}, u32[]{:S(2)}) collective-permute-start(bf16[1,4,32,1024]{3,2,1,0:T(8,128)(2,1)S(1)} %copy-done.94), channel_id=1, source_target_pairs={{0,2},{2,0},{4,6},{6,4},{8,10},{10,8},{12,14},{14,12},{16,18},{18,... | collective-permute-start | bytes 786440 | tf_op jit(solution)/shard_map/ppermute | solution.py:55
  460.6 25.9 %collective-permute-start.73 = (bf16[1,4,32,1024]{3,2,1,0:T(8,128)(2,1)S(1)}, bf16[1,4,32,1024]{3,2,1,0:T(8,128)(2,1)S(1)}, u32[]{:S(2)}, u32[]{:S(2)}) collective-permute-start(bf16[1,4,32,1024]{3,2,1,0:T(8,128)(2,1)S(1)} %copy-done.93), channel_id=1, source_target_pairs={{0,4},{2,6},{4,0},{6,2},{8,12},{10,14},{12,8},{14,10},{16,20},{18,... | collective-permute-start | bytes 786440 | tf_op jit(solution)/shard_map/ppermute | solution.py:55
  484.8 24.6 %collective-permute-start.94 = (bf16[256,1024]{1,0:T(8,128)(2,1)S(1)}, bf16[256,1024]{1,0:T(8,128)(2,1)S(1)}, u32[]{:S(2)}, u32[]{:S(2)}) collective-permute-start(bf16[256,1024]{1,0:T(8,128)(2,1)S(1)} %fusion.20), channel_id=1, source_target_pairs={{0,16},{2,18},{4,20},{6,22},{8,24},{10,26},{12,28},{14,30},{16,0},... | collective-permute-start | bytes 1572872 | tf_op jit(solution)/shard_map/ppermute | solution.py:45
  (201 other events, 1743.3 us)
